TPU v7x, 32 devices: a whole 2x2x4 slice. The times are simulated.
32 devices in a mesh: utt: 8 (over z, y), sp: 4 (over x, core).
Axes of the slice: x: 2, y: 2, z: 4, core: 2. Of those that a mesh axis runs over, the one named last changes fastest.
Arguments:
- frames: bfloat16 [8192, 1024], P(('utt', 'sp')), may hold values from -6 to 6
- skip_frames: bfloat16 [8192, 1024], P(('utt', 'sp')), may hold values from -6 to 6
- lengths: int32 [8, 3], P('utt'), may hold values from 1 to 768, 1024 in all within a row
- flow_time: float32 [8, 3], P('utt'), may hold values from 0 to 1
- skip_weight: bfloat16 [2048, 1024], P(('utt', 'sp')), may hold values from -0.125 to 0.125
- adaln_weight: bfloat16 [1024, 6144], P(('utt', 'sp')), may hold values from -0.1875 to 0.1875
- adaln_bias: bfloat16 [6144], P(('utt', 'sp')), may hold values from -3 to 3
- qkv_weight: bfloat16 [1024, 3072], P(('utt', 'sp')), may hold values from -0.1875 to 0.1875
- qkv_bias: bfloat16 [3072], P(('utt', 'sp')), may hold values from -3 to 3
- output_weight: bfloat16 [1024, 1024], P(('utt', 'sp')), may hold values from -1.5 to 1.5
- output_bias: bfloat16 [1024], P(('utt', 'sp')), may hold values from -3 to 3
- up_weight: bfloat16 [1024, 4096], P(('utt', 'sp')), may hold values from -0.1875 to 0.1875
- up_bias: bfloat16 [4096], P(('utt', 'sp')), may hold values from -3 to 3
- down_weight: bfloat16 [4096, 1024], P(('utt', 'sp')), may hold values from -0.09375 to 0.09375
- down_bias: bfloat16 [1024], P(('utt', 'sp')), may hold values from -3 to 3
- out_grad: bfloat16 [8192, 1024], P(('utt', 'sp')), may hold values from -6 to 6
Outputs:
- mixed_out: bfloat16 [8192, 1024], P(('utt', 'sp'))
- frames_grad: float32 [8192, 1024], P(('utt', 'sp'))
- skip_grad: float32 [8192, 1024], P(('utt', 'sp'))
- skip_weight_grad: float32 [2048, 1024], P(('utt', 'sp'))
- adaln_weight_grad: float32 [1024, 6144], P(('utt', 'sp'))
- adaln_bias_grad: float32 [6144], P(('utt', 'sp'))
- qkv_weight_grad: float32 [1024, 3072], P(('utt', 'sp'))
- qkv_bias_grad: float32 [3072], P(('utt', 'sp'))
- output_weight_grad: float32 [1024, 1024], P(('utt', 'sp'))
- output_bias_grad: float32 [1024], P(('utt', 'sp'))
- up_weight_grad: float32 [1024, 4096], P(('utt', 'sp'))
- up_bias_grad: float32 [4096], P(('utt', 'sp'))
- down_weight_grad: float32 [4096, 1024], P(('utt', 'sp'))
- down_bias_grad: float32 [1024], P(('utt', 'sp'))
Inputs may be any that keep to these rules, and one draw needn't show every extreme that they name: lengths[g] holds the frame counts of the 3 utterances packed in order into group g's 1024 rows; they sum to 1024, and the largest of every row is exactly 768.
All inputs are finite; a program needn't handle non-finite values.
Results may differ from a plain program's by a relative error of at most 0.015.
Values may be sent and summed in bfloat16 or wider, within the bound.
No kernel may reach another device: no remote copies, remote signals or barrier semaphores. Data moves between devices by JAX's collectives and lax.ppermute only.
A program may use at most 256 MiB of HBM per device.

v0:
```python
import math

import jax
import jax.numpy as jnp
from jax import lax
from jax.sharding import PartitionSpec as P

HD = 64


highest_precision = lax.Precision.HIGHEST
mask_value = -1e30


def layer_norm(values):
    mean_row = jnp.mean(values, axis=-1, keepdims=True)
    centered = values - mean_row
    variance = jnp.mean(centered * centered, axis=-1, keepdims=True)
    return centered * lax.rsqrt(variance + 1e-06)


def gelu_tanh(values):
    return jax.nn.gelu(values, approximate=True)


def time_features(flow_row, model_width):
    half_width = model_width // 2
    steps_row = jnp.arange(half_width, dtype=jnp.float32)
    frequency = jnp.exp(steps_row * (-math.log(10000.0) / (half_width - 1)))
    phase_arg = 1000.0 * flow_row[:, None] * frequency[None, :]
    return jnp.concatenate([jnp.sin(phase_arg), jnp.cos(phase_arg)], axis=1)


def rotary(values, position, head_size, direction):
    row_count = values.shape[0]
    col_count = values.shape[1]
    half_head = head_size // 2
    head_count = col_count // head_size
    inverse = jnp.exp(
        jnp.arange(half_head, dtype=jnp.float32) * (-2.0 * math.log(10000.0) / head_size)
    )
    angle_arg = position.astype(jnp.float32)[:, None] * inverse[None, :]
    cosine = jnp.cos(angle_arg)
    sine_row = jnp.sin(angle_arg) * direction
    cos_full = jnp.tile(jnp.concatenate([cosine, cosine], axis=1), (1, head_count))
    sin_full = jnp.tile(jnp.concatenate([-sine_row, sine_row], axis=1), (1, head_count))
    halves = values.reshape(row_count, head_count, 2, half_head)
    swapped = jnp.concatenate([halves[:, :, 1:], halves[:, :, :1]], axis=2).reshape(
        row_count, col_count
    )
    return values * cos_full + swapped * sin_full


def utterance_layout(lengths_row, first_row, row_count):
    ends_at = jnp.cumsum(lengths_row)
    starts_at = ends_at - lengths_row
    frame_ids = first_row + jnp.arange(row_count, dtype=jnp.int32)
    inside = (frame_ids[:, None] >= starts_at[None, :]) & (frame_ids[:, None] < ends_at[None, :])
    segment = jnp.sum(jnp.where(frame_ids[:, None] >= ends_at[None, :], 1, 0), axis=1).astype(
        jnp.int32
    )
    position = frame_ids - jnp.sum(jnp.where(inside, starts_at[None, :], 0), axis=1)
    return (inside, segment, position)


def block_rows():
    return 512


def head_scores(query_block, keys_all, segment_block, segment_all, score_scale):
    scores = (
        jnp.einsum("qhd,khd->hqk", query_block, keys_all, preferred_element_type=jnp.float32)
        * score_scale
    )
    same_seg = segment_block[:, None] == segment_all[None, :]
    return jnp.where(same_seg[None], scores, mask_value)


def attend(query_heads, key_heads, value_heads, segment_all):
    total_rows, col_count = query_heads.shape
    head_count = col_count // HD
    block_size = block_rows()
    block_count = total_rows // block_size
    keys_all = key_heads.reshape(total_rows, head_count, HD)
    values_all = value_heads.reshape(total_rows, head_count, HD)
    score_scale = HD ** (-0.5)

    def one_block(pieces):
        query_block, segment_block = pieces
        masked = head_scores(query_block, keys_all, segment_block, segment_all, score_scale)
        row_max = jnp.max(masked, axis=-1, keepdims=True)
        exp_rows = jnp.exp(masked - row_max)
        totals = jnp.sum(exp_rows, axis=-1, keepdims=True)
        prob_rows = (exp_rows / totals).astype(jnp.bfloat16)
        block_out = jnp.einsum(
            "hqk,khd->qhd", prob_rows, values_all, preferred_element_type=jnp.float32
        )
        return (
            block_out.astype(jnp.bfloat16).reshape(block_size, col_count),
            (row_max + jnp.log(totals))[..., 0],
        )

    outputs, log_totals = lax.map(
        one_block,
        (
            query_heads.reshape(block_count, block_size, head_count, HD),
            segment_all.reshape(block_count, block_size),
        ),
    )
    return (outputs.reshape(total_rows, col_count), log_totals)


def attend_back(query_heads, key_heads, value_heads, grad_heads, log_totals, segment_all):
    total_rows, col_count = query_heads.shape
    head_count = col_count // HD
    block_size = block_rows()
    block_count = total_rows // block_size
    keys_all = key_heads.reshape(total_rows, head_count, HD)
    values_all = value_heads.reshape(total_rows, head_count, HD)
    score_scale = HD ** (-0.5)

    def one_block(carried, pieces):
        key_sum, value_sum = carried
        query_block, grad_block, log_block, segment_block = pieces
        masked = head_scores(query_block, keys_all, segment_block, segment_all, score_scale)
        prob_rows = jnp.exp(masked - log_block[:, :, None])
        grad_probs = jnp.einsum(
            "qhd,khd->hqk", grad_block, values_all, preferred_element_type=jnp.float32
        )
        inner_sum = jnp.sum(prob_rows * grad_probs, axis=-1, keepdims=True)
        grad_scores = (prob_rows * (grad_probs - inner_sum)).astype(jnp.bfloat16)
        grad_query = (
            jnp.einsum("hqk,khd->qhd", grad_scores, keys_all, preferred_element_type=jnp.float32)
            * score_scale
        )
        key_sum = (
            key_sum
            + jnp.einsum(
                "hqk,qhd->khd", grad_scores, query_block, preferred_element_type=jnp.float32
            )
            * score_scale
        )
        value_sum = value_sum + jnp.einsum(
            "hqk,qhd->khd",
            prob_rows.astype(jnp.bfloat16),
            grad_block,
            preferred_element_type=jnp.float32,
        )
        return (
            (key_sum, value_sum),
            grad_query.astype(jnp.bfloat16).reshape(block_size, col_count),
        )

    zero_sums = jnp.zeros((total_rows, head_count, HD), jnp.float32)
    (key_sum, value_sum), query_grads = lax.scan(
        one_block,
        (zero_sums, zero_sums),
        (
            query_heads.reshape(block_count, block_size, head_count, HD),
            grad_heads.reshape(block_count, block_size, head_count, HD),
            log_totals,
            segment_all.reshape(block_count, block_size),
        ),
    )
    return (
        query_grads.reshape(total_rows, col_count),
        key_sum.astype(jnp.bfloat16).reshape(total_rows, col_count),
        value_sum.astype(jnp.bfloat16).reshape(total_rows, col_count),
    )


def column_grad(left, right):
    return jnp.einsum("fi,fo->io", left, right, preferred_element_type=jnp.float32)


def body(
    frames,
    skip_frames,
    lengths,
    flow_time,
    skip_weight,
    adaln_weight,
    adaln_bias,
    qkv_weight,
    qkv_bias,
    output_weight,
    output_bias,
    up_weight,
    up_bias,
    down_weight,
    down_bias,
    out_grad,
):
    row_count, model_width = frames.shape
    sp_size = lax.axis_size("sp")
    group_rows = row_count * sp_size
    lengths_row = lengths[0]
    inside, segment_own, position = utterance_layout(
        lengths_row, lax.axis_index("sp") * row_count, row_count
    )
    onehot = inside.astype(jnp.float32)
    silu_time = jax.nn.silu(time_features(flow_time[0], model_width)).astype(jnp.bfloat16)
    full_skip, full_adaln, full_adaln_bias, full_qkv, full_qkv_bias = (
        lax.all_gather(skip_weight, ("utt", "sp"), axis=0, tiled=True),
        lax.all_gather(adaln_weight, ("utt", "sp"), axis=0, tiled=True),
        lax.all_gather(adaln_bias, ("utt", "sp"), axis=0, tiled=True),
        lax.all_gather(qkv_weight, ("utt", "sp"), axis=0, tiled=True),
        lax.all_gather(qkv_bias, ("utt", "sp"), axis=0, tiled=True),
    )
    mod_table = (
        jnp.dot(silu_time, full_adaln, preferred_element_type=jnp.float32)
        + full_adaln_bias.astype(jnp.float32)[None, :]
    )
    modulation = jnp.dot(
        onehot, mod_table, precision=highest_precision, preferred_element_type=jnp.float32
    )
    shift_attn, scale_attn, gate_attn, shift_ffn, scale_ffn, gate_ffn = jnp.split(
        modulation, 6, axis=1
    )
    joined = jnp.concatenate([frames, skip_frames], axis=1)
    base_rows = jnp.dot(joined, full_skip, preferred_element_type=jnp.float32)
    base_norm, base_pull = jax.vjp(layer_norm, base_rows)
    normed = (base_norm * (1.0 + scale_attn) + shift_attn).astype(jnp.bfloat16)
    projected = (
        jnp.dot(normed, full_qkv, preferred_element_type=jnp.float32)
        + full_qkv_bias.astype(jnp.float32)[None, :]
    )
    query_rows = rotary(projected[:, :model_width], position, HD, 1.0).astype(jnp.bfloat16)
    key_rows = rotary(projected[:, model_width : 2 * model_width], position, HD, 1.0).astype(
        jnp.bfloat16
    )
    value_rows = projected[:, 2 * model_width :].astype(jnp.bfloat16)
    query_heads, key_heads, value_heads = (
        lax.all_to_all(query_rows, "sp", split_axis=1, concat_axis=0, tiled=True),
        lax.all_to_all(key_rows, "sp", split_axis=1, concat_axis=0, tiled=True),
        lax.all_to_all(value_rows, "sp", split_axis=1, concat_axis=0, tiled=True),
    )
    layout_all = utterance_layout(lengths_row, 0, group_rows)
    segment_all = layout_all[1]
    attended_heads, log_totals = attend(query_heads, key_heads, value_heads, segment_all)
    attended = lax.all_to_all(attended_heads, "sp", split_axis=0, concat_axis=1, tiled=True)
    full_output, full_output_bias, full_up, full_up_bias, full_down, full_down_bias = (
        lax.all_gather(output_weight, ("utt", "sp"), axis=0, tiled=True),
        lax.all_gather(output_bias, ("utt", "sp"), axis=0, tiled=True),
        lax.all_gather(up_weight, ("utt", "sp"), axis=0, tiled=True),
        lax.all_gather(up_bias, ("utt", "sp"), axis=0, tiled=True),
        lax.all_gather(down_weight, ("utt", "sp"), axis=0, tiled=True),
        lax.all_gather(down_bias, ("utt", "sp"), axis=0, tiled=True),
    )
    branch = (
        jnp.dot(attended, full_output, preferred_element_type=jnp.float32)
        + full_output_bias.astype(jnp.float32)[None, :]
    )
    middle = base_rows + gate_attn * branch
    middle_norm, middle_pull = jax.vjp(layer_norm, middle)
    normed_ffn = (middle_norm * (1.0 + scale_ffn) + shift_ffn).astype(jnp.bfloat16)
    hidden = (
        jnp.dot(normed_ffn, full_up, preferred_element_type=jnp.float32)
        + full_up_bias.astype(jnp.float32)[None, :]
    )
    active = gelu_tanh(hidden).astype(jnp.bfloat16)
    result = (
        jnp.dot(active, full_down, preferred_element_type=jnp.float32)
        + full_down_bias.astype(jnp.float32)[None, :]
    )
    mixed_out = (middle + gate_ffn * result).astype(jnp.bfloat16)
    grad_out = out_grad.astype(jnp.float32)
    back_output, back_up, back_up_bias, back_down = (
        lax.all_gather(output_weight, ("utt", "sp"), axis=0, tiled=True),
        lax.all_gather(up_weight, ("utt", "sp"), axis=0, tiled=True),
        lax.all_gather(up_bias, ("utt", "sp"), axis=0, tiled=True),
        lax.all_gather(down_weight, ("utt", "sp"), axis=0, tiled=True),
    )
    hidden_again = (
        jnp.dot(normed_ffn, back_up, preferred_element_type=jnp.float32)
        + back_up_bias.astype(jnp.float32)[None, :]
    )
    active_again, gelu_pull = jax.vjp(gelu_tanh, hidden_again)
    active_low = active_again.astype(jnp.bfloat16)
    grad_gate_ffn = grad_out * result
    grad_result = (gate_ffn * grad_out).astype(jnp.bfloat16)
    grad_down = column_grad(active_low, grad_result)
    grad_down_bias = jnp.sum(grad_result.astype(jnp.float32), axis=0)
    grad_active = jnp.dot(grad_result, back_down.T, preferred_element_type=jnp.float32)
    grad_hidden = gelu_pull(grad_active)[0].astype(jnp.bfloat16)
    grad_up = column_grad(normed_ffn, grad_hidden)
    grad_up_bias = jnp.sum(grad_hidden.astype(jnp.float32), axis=0)
    grad_normed_ffn = jnp.dot(grad_hidden, back_up.T, preferred_element_type=jnp.float32)
    grad_scale_ffn = grad_normed_ffn * middle_norm
    grad_middle = grad_out + middle_pull(grad_normed_ffn * (1.0 + scale_ffn))[0]
    grad_gate_attn = grad_middle * branch
    grad_branch = (gate_attn * grad_middle).astype(jnp.bfloat16)
    grad_output = column_grad(attended, grad_branch)
    grad_output_bias = jnp.sum(grad_branch.astype(jnp.float32), axis=0)
    grad_attended = jnp.dot(grad_branch, back_output.T, preferred_element_type=jnp.float32).astype(
        jnp.bfloat16
    )
    post_sums = (
        lax.psum_scatter(grad_output, ("utt", "sp"), scatter_dimension=0, tiled=True),
        lax.psum_scatter(grad_output_bias, ("utt", "sp"), scatter_dimension=0, tiled=True),
        lax.psum_scatter(grad_up, ("utt", "sp"), scatter_dimension=0, tiled=True),
        lax.psum_scatter(grad_up_bias, ("utt", "sp"), scatter_dimension=0, tiled=True),
        lax.psum_scatter(grad_down, ("utt", "sp"), scatter_dimension=0, tiled=True),
        lax.psum_scatter(grad_down_bias, ("utt", "sp"), scatter_dimension=0, tiled=True),
    )
    grad_heads = lax.all_to_all(grad_attended, "sp", split_axis=1, concat_axis=0, tiled=True)
    query_grad_heads, key_grad_heads, value_grad_heads = attend_back(
        query_heads, key_heads, value_heads, grad_heads, log_totals, segment_all
    )
    grad_query, grad_key, grad_value = (
        lax.all_to_all(query_grad_heads, "sp", split_axis=0, concat_axis=1, tiled=True),
        lax.all_to_all(key_grad_heads, "sp", split_axis=0, concat_axis=1, tiled=True),
        lax.all_to_all(value_grad_heads, "sp", split_axis=0, concat_axis=1, tiled=True),
    )
    back_skip, back_qkv = (
        lax.all_gather(skip_weight, ("utt", "sp"), axis=0, tiled=True),
        lax.all_gather(qkv_weight, ("utt", "sp"), axis=0, tiled=True),
    )
    grad_projected = jnp.concatenate(
        [
            rotary(grad_query.astype(jnp.float32), position, HD, -1.0),
            rotary(grad_key.astype(jnp.float32), position, HD, -1.0),
            grad_value.astype(jnp.float32),
        ],
        axis=1,
    ).astype(jnp.bfloat16)
    grad_qkv = column_grad(normed, grad_projected)
    grad_qkv_bias = jnp.sum(grad_projected.astype(jnp.float32), axis=0)
    grad_normed = jnp.dot(grad_projected, back_qkv.T, preferred_element_type=jnp.float32)
    grad_scale_attn = grad_normed * base_norm
    grad_base = (grad_middle + base_pull(grad_normed * (1.0 + scale_attn))[0]).astype(jnp.bfloat16)
    grad_skip_weight = column_grad(joined, grad_base)
    grad_joined = jnp.dot(grad_base, back_skip.T, preferred_element_type=jnp.float32)
    grad_modulation = jnp.concatenate(
        [
            grad_normed,
            grad_scale_attn,
            grad_gate_attn,
            grad_normed_ffn,
            grad_scale_ffn,
            grad_gate_ffn,
        ],
        axis=1,
    )
    grad_table = jnp.einsum(
        "fu,fc->uc",
        onehot,
        grad_modulation,
        precision=highest_precision,
        preferred_element_type=jnp.float32,
    )
    grad_adaln = jnp.einsum(
        "ud,uc->dc",
        silu_time.astype(jnp.float32),
        grad_table,
        precision=highest_precision,
        preferred_element_type=jnp.float32,
    )
    grad_adaln_bias = jnp.sum(grad_table, axis=0)
    skip_sum, adaln_sum, adaln_bias_sum, qkv_sum, qkv_bias_sum = (
        lax.psum_scatter(grad_skip_weight, ("utt", "sp"), scatter_dimension=0, tiled=True),
        lax.psum_scatter(grad_adaln, ("utt", "sp"), scatter_dimension=0, tiled=True),
        lax.psum_scatter(grad_adaln_bias, ("utt", "sp"), scatter_dimension=0, tiled=True),
        lax.psum_scatter(grad_qkv, ("utt", "sp"), scatter_dimension=0, tiled=True),
        lax.psum_scatter(grad_qkv_bias, ("utt", "sp"), scatter_dimension=0, tiled=True),
    )
    return (
        mixed_out,
        grad_joined[:, :model_width],
        grad_joined[:, model_width:],
        skip_sum,
        adaln_sum,
        adaln_bias_sum,
        qkv_sum,
        qkv_bias_sum,
        post_sums[0],
        post_sums[1],
        post_sums[2],
        post_sums[3],
        post_sums[4],
        post_sums[5],
    )


def solution(mesh):
    return jax.shard_map(
        body,
        mesh=mesh,
        in_specs=(
            P(("utt", "sp"), None),
            P(("utt", "sp"), None),
            P("utt", None),
            P("utt", None),
            P(("utt", "sp"), None),
            P(("utt", "sp"), None),
            P(("utt", "sp")),
            P(("utt", "sp"), None),
            P(("utt", "sp")),
            P(("utt", "sp"), None),
            P(("utt", "sp")),
            P(("utt", "sp"), None),
            P(("utt", "sp")),
            P(("utt", "sp"), None),
            P(("utt", "sp")),
            P(("utt", "sp"), None),
        ),
        out_specs=(
            P(("utt", "sp"), None),
            P(("utt", "sp"), None),
            P(("utt", "sp"), None),
            P(("utt", "sp"), None),
            P(("utt", "sp"), None),
            P(("utt", "sp")),
            P(("utt", "sp"), None),
            P(("utt", "sp")),
            P(("utt", "sp"), None),
            P(("utt", "sp")),
            P(("utt", "sp"), None),
            P(("utt", "sp")),
            P(("utt", "sp"), None),
            P(("utt", "sp")),
        ),
        check_vma=False,
    )
```

profile of v0, /device:TPU:4, one launch (start us, length us, event | category | flops | bytes accessed | tf_op | source)
XLA Modules:
  0.0 1586.2 jit_solution(5215454053969696517)
XLA Ops:
  14.6 41.9 %all-reduce.10 = (bf16[6144]{0:T(1024)(128)(2,1)S(1)}, bf16[3072]{0:T(1024)(128)(2,1)S(1)}, bf16[1024]{0:T(1024)(128)(2,1)S(1)}, bf16[1024]{0:T(1024)(128)(2,1)S(1)}) all-reduce(bf16[6144]{0:T(1024)(128)(2,1)S(1)} %dynamic-update-slice, bf16[3072]{0:T(1024)(128)(2,1)S(1)} %dynamic-update-slice.1, ...), channel_id=1, replica_groups=mesh['utt'=8,'sp'=4] {'utt','sp'}, use_global_device_ids=true, to_apply=%add | all-reduce | flops 11264 | bytes 45056
  63.2 11.0 all-gather.8.cloned.1.call-done
  78.3 93.3 %all-gather.10.cloned.1.call-done = bf16[1024,6144]{1,0:T(8,128)(2,1)} async-done(((bf16[32,6144]{1,0:T(8,128)(2,1)}), bf16[1024,6144]{1,0:T(8,128)(2,1)}) %all-gather.10.cloned.1.call-update) | async-done | bytes 12582928 | tf_op jit(solution)/shard_map/all_gather | solution.py:205
  171.7 6.3 convolution_add_fusion
  183.7 58.6 %all-gather.12.cloned.1.call-done = bf16[1024,3072]{1,0:T(8,128)(2,1)} async-done(((bf16[32,3072]{1,0:T(8,128)(2,1)}), bf16[1024,3072]{1,0:T(8,128)(2,1)}) %all-gather.12.cloned.1.call-update) | async-done | bytes 6291472 | tf_op jit(solution)/shard_map/all_gather | solution.py:207
  274.0 8.0 all-to-all-done
  287.6 8.6 all-to-all-done.1
  303.2 5.4 all-to-all-done.2
  310.1 16.5 %while.27 = (s32[]{:T(128)}, bf16[2,512,256]{2,1,0:T(8,128)(2,1)}, f32[2,4,512]{2,1,0:T(4,128)S(1)}, s32[2,512]{1,0:T(2,128)S(1)}, s32[1024]{0:T(1024)S(1)}, /*i...) while((s32[]{:T(128)}, bf16[2,512,256]{2,1,0:T(8,128)(2,1)}, ...), condition=%wide.region_8.9_spmd, body=%wide.region_5.8_spmd.sunk | while | flops 562690048 | bytes 29960808 | solution.py:103
  330.0 43.3 %all-gather = bf16[32,1,128]{2,1,0:T(2,128)(2,1)S(1)} all-gather(bf16[1,1,128]{2,1,0:T(2,128)(2,1)S(1)} %bitcast.228), channel_id=1, replica_groups=mesh['utt'=8,'sp'=4] {'utt','sp'}, dimensions={0}, use_global_device_ids=true | all-gather | bytes 8448 | tf_op jit(solution)/shard_map/all_gather | solution.py:246
  387.1 7.7 fusion.84
  394.9 71.1 %all-gather.16.cloned.1.call-done = bf16[1024,4096]{1,0:T(8,128)(2,1)} async-done(((bf16[32,4096]{1,0:T(8,128)(2,1)}), bf16[1024,4096]{1,0:T(8,128)(2,1)}) %all-gather.16.cloned.1.call-update) | async-done | bytes 8388624 | tf_op jit(solution)/shard_map/all_gather | solution.py:245
  466.0 8.9 convert_reduce_fusion
  474.9 8.5 multiply_reduce_fusion.2
  483.5 5.8 fusion.74
  514.6 40.7 %while.28 = (s32[]{:T(128)}, f32[1024,4,64]{0,2,1:T(8,128)S(1)}, f32[1024,4,64]{0,2,1:T(8,128)}, bf16[2,512,256]{2,1,0:T(8,128)(2,1)}, bf16[2,512,4,64]{1,3,2,0:...) while((s32[]{:T(128)}, f32[1024,4,64]{0,2,1:T(8,128)S(1)}, ...), condition=%wide.region_15.16_spmd.clone, body=%wide.region_13.15_spmd.clone.sunk | while | flops 1375729664 | bytes 165481328 | solution.py:155
  560.2 10.3 all-to-all-done.5
  577.0 7.7 all-to-all-done.6
  589.8 9.6 all-to-all-done.7
  599.4 7.4 fusion.68
  608.1 6.0 constant_dynamic-update-slice_fusion.5
  618.3 6.1 fusion.86
  625.5 9.7 fusion.88
  636.3 10.8 fusion.70
  653.4 5.2 fusion.83
  658.6 13.4 fusion.65
  672.8 43.6 %all-reduce.9 = (f32[6144]{0:T(1024)S(1)}, f32[3072]{0:T(1024)S(1)}, f32[1024]{0:T(1024)S(1)}, f32[4096]{0:T(1024)S(1)}, f32[1024]{0:T(1024)S(1)}) all-reduce(f32[6144]{0:T(1024)S(1)} %get-tuple-element.353, f32[3072]{0:T(1024)S(1)} %convert_reduce_fusion.1, ...), channel_id=4, replica_groups=mesh['utt'=8,'sp'=4] {'utt','sp'}, use_global_device_ids=true, to_apply=%region_21.22.clone | all-reduce | flops 15360 | bytes 122880
  724.4 79.4 %reduce-scatter.11.cloned.1.call-done = f32[32,3072]{1,0:T(8,128)} async-done(((f32[1024,3072]{1,0:T(8,128)}), f32[32,3072]{1,0:T(8,128)}) %reduce-scatter.11.cloned.1.call-update) | async-done | bytes 393232 | tf_op jit(solution)/shard_map/reduce_scatter | solution.py:364
  803.9 141.5 %reduce-scatter.7.cloned.1.call-done = f32[64,1024]{1,0:T(8,128)} async-done(((f32[2048,1024]{1,0:T(8,128)}), f32[64,1024]{1,0:T(8,128)}) %reduce-scatter.7.cloned.1.call-update) | async-done | bytes 262160 | tf_op jit(solution)/shard_map/reduce_scatter | solution.py:361
  945.3 189.2 %reduce-scatter.15.cloned.1.call-done = f32[32,4096]{1,0:T(8,128)} async-done(((f32[1024,4096]{1,0:T(8,128)}), f32[32,4096]{1,0:T(8,128)}) %reduce-scatter.15.cloned.1.call-update) | async-done | bytes 524304 | tf_op jit(solution)/shard_map/reduce_scatter | solution.py:301
  1134.5 187.5 %reduce-scatter.17.cloned.1.call-done = f32[128,1024]{1,0:T(8,128)} async-done(((f32[4096,1024]{1,0:T(8,128)}), f32[128,1024]{1,0:T(8,128)}) %reduce-scatter.17.cloned.1.call-update) | async-done | bytes 524304 | tf_op jit(solution)/shard_map/reduce_scatter | solution.py:303
  1322.0 256.9 %reduce-scatter.9.cloned.1.call-done = f32[32,6144]{1,0:T(8,128)} async-done(((f32[1024,6144]{1,0:T(8,128)}), f32[32,6144]{1,0:T(8,128)}) %reduce-scatter.9.cloned.1.call-update) | async-done | bytes 786448 | tf_op jit(solution)/shard_map/reduce_scatter | solution.py:362
  (331 shorter events, 207.6 us)
Async XLA Ops:
  7.2 67.0 %all-gather.8.cloned.1.call-start = ((), (), s32[]{:S(2)}) async-start(), calls=%async_computation.14 | async-start | bytes 4325376 | tf_op jit(solution)/shard_map/all_gather | solution.py:204
  7.9 163.7 %all-gather.10.cloned.1.call-start = ((), (), s32[]{:S(2)}) async-start(), calls=%async_computation.15 | async-start | bytes 12976128 | tf_op jit(solution)/shard_map/all_gather | solution.py:205
  8.7 233.7 %all-gather.12.cloned.1.call-start = ((), (), s32[]{:S(2)}) async-start(), calls=%async_computation.16 | async-start | bytes 6488064 | tf_op jit(solution)/shard_map/all_gather | solution.py:207
  9.4 366.0 %all-gather.14.cloned.1.call-start = ((), (), s32[]{:S(2)}) async-start(), calls=%async_computation.17 | async-start | bytes 2162688 | tf_op jit(solution)/shard_map/all_gather | solution.py:243
  10.0 377.2 %all-gather.18.cloned.1.call-start = ((), (), s32[]{:S(2)}) async-start(), calls=%async_computation.19 | async-start | bytes 8650752 | tf_op jit(solution)/shard_map/all_gather | solution.py:247
  10.6 455.4 %all-gather.16.cloned.1.call-start = ((), (), s32[]{:S(2)}) async-start(), calls=%async_computation.18 | async-start | bytes 8650752 | tf_op jit(solution)/shard_map/all_gather | solution.py:245
  56.5 121.5 %copy-start.51 = (s32[256]{0:T(256)}, s32[256]{0:T(256)S(1)}, u32[]{:S(2)}) copy-start(s32[256]{0:T(256)S(1)} %iota_add_fusion) | copy-start | bytes 3076
  57.3 242.4 %copy-start.59 = (s32[3,1]{0,1:T(1,128)}, s32[3,1]{0,1:T(1,128)S(1)}, u32[]{:S(2)}) copy-start(s32[3,1]{0,1:T(1,128)S(1)} %reduce-window.4) | copy-start | bytes 40
  58.0 120.0 %copy-start.61 = (s32[3]{0:T(128)}, s32[3]{0:T(128)S(1)}, u32[]{:S(2)}) copy-start(s32[3]{0:T(128)S(1)} %fusion.62) | copy-start | bytes 40
  63.2 108.5 %copy-start.40 = (f32[3,512]{1,0:T(4,128)}, f32[3,512]{1,0:T(4,128)S(1)}, u32[]{:S(2)}) copy-start(f32[3,512]{1,0:T(4,128)S(1)} %get-tuple-element.338) | copy-start | bytes 18436
  63.2 108.5 %copy-start.42 = (f32[3,512]{1,0:T(4,128)}, f32[3,512]{1,0:T(4,128)S(1)}, u32[]{:S(2)}) copy-start(f32[3,512]{1,0:T(4,128)S(1)} %get-tuple-element.339) | copy-start | bytes 18436
  78.0 297.4 %copy-start.6 = (f32[256,1024]{1,0:T(8,128)}, f32[256,1024]{1,0:T(8,128)S(1)}, u32[]{:S(2)}) copy-start(f32[256,1024]{1,0:T(8,128)S(1)} %get-tuple-element.346) | copy-start | bytes 3145732
  78.0 102.7 %copy-start.47 = (f32[256]{0:T(256)}, f32[256]{0:T(256)S(1)}, u32[]{:S(2)}) copy-start(f32[256]{0:T(256)S(1)} %broadcast_multiply_fusion.1) | copy-start | bytes 3076
  78.3 93.4 %copy-start.57 = (f32[256]{0:T(256)}, f32[256]{0:T(256)S(1)}, u32[]{:S(2)}) copy-start(f32[256]{0:T(256)S(1)} %multiply_reduce_fusion.4) | copy-start | bytes 3076
  78.3 102.4 %copy-start.53 = (f32[256]{0:T(256)}, f32[256]{0:T(256)S(1)}, u32[]{:S(2)}) copy-start(f32[256]{0:T(256)S(1)} %fusion.60) | copy-start | bytes 3076
  269.4 12.6 all-to-all-start
  282.0 14.2 all-to-all-start.1
  296.3 12.3 all-to-all-start.2
  326.5 46.8 %all-to-all-start.3 = ((bf16[4,256,256]{2,1,0:T(8,128)(2,1)}), bf16[4,256,256]{2,1,0:T(8,128)(2,1)S(1)}, u32[]{:S(2)}, u32[]{:S(2)}) async-start(bf16[4,256,256]{2,1,0:T(8,128)(2,1)} %bitcast.219), calls=%async_computation.3 | async-start | bytes 1048576 | tf_op jit(solution)/shard_map/all_to_all | solution.py:241
  379.1 104.3 %copy-start.49 = (f32[256]{0:T(256)}, f32[256]{0:T(256)S(1)}, u32[]{:S(2)}) copy-start(f32[256]{0:T(256)S(1)} %broadcast_multiply_fusion) | copy-start | bytes 3076
  380.2 103.3 %copy-start.55 = (f32[256]{0:T(256)}, f32[256]{0:T(256)S(1)}, u32[]{:S(2)}) copy-start(f32[256]{0:T(256)S(1)} %fusion.61) | copy-start | bytes 3076
  383.1 82.9 %copy-start.23 = (bf16[256,1024]{1,0:T(8,128)(2,1)}, bf16[256,1024]{1,0:T(8,128)(2,1)S(1)}, u32[]{:S(2)}) copy-start(bf16[256,1024]{1,0:T(8,128)(2,1)S(1)} %get-tuple-element.316) | copy-start | bytes 1572868
  496.2 13.1 all-to-all-start.4
  500.4 224.0 %reduce-scatter.13.cloned.1.call-start = ((), (), s32[]{:S(2)}) async-start(), calls=%async_computation.23 | async-start | bytes 4325376 | tf_op jit(solution)/shard_map/reduce_scatter | solution.py:299
  555.3 15.2 all-to-all-start.5
  570.5 14.1 all-to-all-start.6
  584.7 14.8 all-to-all-start.7
  588.2 215.7 %reduce-scatter.11.cloned.1.call-start = ((), (), s32[]{:S(2)}) async-start(), calls=%async_computation.22 | async-start | bytes 12976128 | tf_op jit(solution)/shard_map/reduce_scatter | solution.py:364
  606.9 338.4 %reduce-scatter.7.cloned.1.call-start = ((), (), s32[]{:S(2)}) async-start(), calls=%async_computation.20 | async-start | bytes 8650752 | tf_op jit(solution)/shard_map/reduce_scatter | solution.py:361
  624.5 510.1 %reduce-scatter.15.cloned.1.call-start = ((), (), s32[]{:S(2)}) async-start(), calls=%async_computation.24 | async-start | bytes 17301504 | tf_op jit(solution)/shard_map/reduce_scatter | solution.py:301
  635.2 686.7 %reduce-scatter.17.cloned.1.call-start = ((), (), s32[]{:S(2)}) async-start(), calls=%async_computation.25 | async-start | bytes 17301504 | tf_op jit(solution)/shard_map/reduce_scatter | solution.py:303
  647.1 931.8 %reduce-scatter.9.cloned.1.call-start = ((), (), s32[]{:S(2)}) async-start(), calls=%async_computation.21 | async-start | bytes 25952256 | tf_op jit(solution)/shard_map/reduce_scatter | solution.py:362
  (61 other events, 490.8 us)
Sparse Core Ops, SparseCore 0:
  10.9 63.2 all-gather.7
  77.0 94.5 all-gather.9
  174.5 67.7 all-gather.11
  245.0 57.4 all-gather.13
  305.2 81.8 all-gather.17
  389.9 76.0 all-gather.15
  504.6 131.4 reduce-scatter.12
  642.7 161.1 reduce-scatter.10
  806.8 138.4 reduce-scatter.6
  948.1 186.3 reduce-scatter.14
  1137.5 184.4 reduce-scatter.16
  1330.0 248.8 reduce-scatter.8
where the time goes:
time: 1600 us; the launch traced here: 1590 us
  waiting for transfers between devices  1150 us (72%)
  matrix products  155 us (10%)
  blocking collectives  129 us (8%)
  local copies, waits for them, and re-layouts  69.7 us (4%)
  other arithmetic  35.7 us (2%)
  starting transfers between devices  30 us (2%)
    reduce_scatter x1, waiting for transfers between devices, body(): lax.psum_scatter(grad_adaln, ('utt', 'sp'), scatter_dimension=0, tiled=True)  257 us
    reduce_scatter x1, waiting for transfers between devices, body(): lax.psum_scatter(grad_up, ('utt', 'sp'), scatter_dimension=0, tiled=True)  189 us
    reduce_scatter x1, waiting for transfers between devices, body(): lax.psum_scatter(grad_down, ('utt', 'sp'), scatter_dimension=0, tiled=True)  187 us
    reduce_scatter x1, waiting for transfers between devices, body(): lax.psum_scatter(grad_skip_weight, ('utt', 'sp'), scatter_dimension=0, ti...  141 us
    all_gather x1, waiting for transfers between devices, body(): lax.all_gather(adaln_weight, ('utt', 'sp'), axis=0, tiled=True)  93.3 us
    unnamed x2, blocking collectives  85.4 us
    reduce_scatter x1, waiting for transfers between devices, body(): lax.psum_scatter(grad_qkv, ('utt', 'sp'), scatter_dimension=0, tiled=True)  79.4 us
    all_gather x1, waiting for transfers between devices, body(): lax.all_gather(up_weight, ('utt', 'sp'), axis=0, tiled=True)  71.1 us
  transfers between devices with their start and end apart: 20, of which 17 were waited for; matrix products, arithmetic and copies ran while one was open for 13% of the time, Pallas kernels for 0%

commit v1 on v0

v1 whole, which is shorter than its diff:
```python
import math

import jax
import jax.numpy as jnp
from jax import lax
from jax.sharding import PartitionSpec as P

HD = 64
LANES = 128
BF = jnp.bfloat16
F32 = jnp.float32
highest_precision = lax.Precision.HIGHEST
mask_value = -1e30


def dot32(left, right):
    return jnp.dot(left, right, preferred_element_type=F32)


def dot_nt(left, right):
    return lax.dot_general(left, right, (((1,), (1,)), ((), ())), preferred_element_type=F32)


def dot_tn(left, right):
    return lax.dot_general(left, right, (((0,), (0,)), ((), ())), preferred_element_type=F32)


def xor_sp(values, distance):
    size = lax.axis_size("sp")
    return lax.ppermute(values, "sp", [(i, i ^ distance) for i in range(size)])


def gather_sp(own):
    size = lax.axis_size("sp")
    blocks = {0: own}
    step = size // 2
    while step >= 1:
        for d in list(blocks):
            blocks[d ^ step] = xor_sp(blocks[d], step)
        step //= 2
    return [blocks[d] for d in range(size)]


def reduce_sp(parts):
    size = lax.axis_size("sp")
    sums = {d: parts[d] for d in range(size)}
    step = 1
    while step < size:
        kept = {}
        for d in sums:
            if d & step == 0:
                arrived = xor_sp(sums[d ^ step].astype(BF), step).astype(F32)
                kept[d] = sums[d] + arrived
        sums = kept
        step *= 2
    return sums[0]


def exchange_sp(parts):
    return [parts[0]] + [xor_sp(parts[d], d) for d in range(1, len(parts))]


def in_device_order(blocks):
    stacked = jnp.stack(blocks)
    me = lax.axis_index("sp")
    return [
        lax.dynamic_index_in_dim(stacked, me ^ a, 0, keepdims=False) for a in range(len(blocks))
    ]


def sum_sp(values):
    size = lax.axis_size("sp")
    step = size // 2
    while step >= 1:
        values = values + xor_sp(values, step)
        step //= 2
    return values


def high_groups():
    high = lax.axis_size("utt") // 2
    return [[z * 2 + y for z in range(high)] for y in range(2)]


def low_partner():
    return [(i, i ^ 1) for i in range(lax.axis_size("utt"))]


def gather_utt(own):
    size = lax.axis_size("utt")
    high = size // 2
    tiled = jnp.broadcast_to(own[None], (high,) + own.shape)
    line = lax.all_to_all(
        tiled, "utt", 0, 0, axis_index_groups=high_groups(), tiled=True
    )
    other = lax.ppermute(line, "utt", low_partner())
    first = lax.axis_index("utt") % 2 == 0
    both = jnp.stack([jnp.where(first, line, other), jnp.where(first, other, line)], axis=1)
    return both.reshape((size,) + own.shape)


def scatter_utt(parts):
    size = lax.axis_size("utt")
    high = size // 2
    low = lax.axis_index("utt") % 2
    pairs = parts.reshape((high, 2) + parts.shape[1:])
    keep = lax.dynamic_index_in_dim(pairs, low, 1, keepdims=False)
    send = lax.dynamic_index_in_dim(pairs, 1 - low, 1, keepdims=False)
    arrived = lax.ppermute(send.astype(BF), "utt", low_partner())
    half = (keep.astype(F32) + arrived.astype(F32)).astype(BF)
    pieces = lax.all_to_all(half, "utt", 0, 0, axis_index_groups=high_groups(), tiled=True)
    return jnp.sum(pieces.astype(F32), axis=0)


def to_owner(values):
    n_u, n_s = lax.axis_size("utt"), lax.axis_size("sp")
    routes = []
    for p in range(n_u):
        for s in range(n_s):
            routes.append((p * n_s + s, s * n_u + p))
    return lax.ppermute(values, ("utt", "sp"), routes)


def owned(values):
    n = lax.axis_size("utt") * lax.axis_size("sp")
    j = lax.axis_index("utt") * lax.axis_size("sp") + lax.axis_index("sp")
    size = values.shape[-1] // n
    return lax.dynamic_slice_in_dim(values, j * size, size, values.ndim - 1)


def norm_parts(values):
    mean_row = jnp.mean(values, axis=-1, keepdims=True)
    centered = values - mean_row
    variance = jnp.mean(centered * centered, axis=-1, keepdims=True)
    scale = lax.rsqrt(variance + 1e-06)
    return centered * scale, scale


def norm_back(normal, scale, grads):
    mean_grad = jnp.mean(grads, axis=-1, keepdims=True)
    mean_both = jnp.mean(grads * normal, axis=-1, keepdims=True)
    return (grads - mean_grad - normal * mean_both) * scale


def gelu_tanh(values):
    return jax.nn.gelu(values, approximate=True)


def rotary(values, position, direction):
    row_count, col_count = values.shape
    half_head = HD // 2
    head_count = col_count // HD
    inverse = jnp.exp(jnp.arange(half_head, dtype=F32) * (-2.0 * math.log(10000.0) / HD))
    angle_arg = position.astype(F32)[:, None] * inverse[None, :]
    cosine = jnp.cos(angle_arg)
    sine_row = jnp.sin(angle_arg) * direction
    cos_full = jnp.tile(jnp.concatenate([cosine, cosine], axis=1), (1, head_count))
    sin_full = jnp.tile(jnp.concatenate([-sine_row, sine_row], axis=1), (1, head_count))
    first = (jnp.arange(col_count) % HD < half_head)[None, :]
    swapped = jnp.where(
        first, jnp.roll(values, -half_head, axis=1), jnp.roll(values, half_head, axis=1)
    )
    return values * cos_full + swapped * sin_full


def utterance_layout(lengths_row, frame_ids):
    ends_at = jnp.cumsum(lengths_row)
    starts_at = ends_at - lengths_row
    inside = (frame_ids[:, None] >= starts_at[None, :]) & (frame_ids[:, None] < ends_at[None, :])
    segment = jnp.sum(jnp.where(frame_ids[:, None] >= ends_at[None, :], 1, 0), axis=1).astype(
        jnp.int32
    )
    position = frame_ids - jnp.sum(jnp.where(inside, starts_at[None, :], 0), axis=1)
    return inside, segment, position


def block_rows():
    return 512


def head_scores(query_block, keys_all, segment_block, segment_all, score_scale):
    scores = jnp.einsum("qhd,khd->hqk", query_block, keys_all, preferred_element_type=F32)
    same_seg = segment_block[:, None] == segment_all[None, :]
    return jnp.where(same_seg[None], scores * score_scale, mask_value)


def attend(query_heads, key_heads, value_heads, segment_all):
    total_rows, col_count = query_heads.shape
    head_count = col_count // HD
    block_size = block_rows()
    block_count = total_rows // block_size
    keys_all = key_heads.reshape(total_rows, head_count, HD)
    values_all = value_heads.reshape(total_rows, head_count, HD)
    score_scale = HD ** (-0.5)

    def one_block(pieces):
        query_block, segment_block = pieces
        masked = head_scores(query_block, keys_all, segment_block, segment_all, score_scale)
        row_max = jnp.max(masked, axis=-1, keepdims=True)
        exp_rows = jnp.exp(masked - row_max)
        totals = jnp.sum(exp_rows, axis=-1, keepdims=True)
        prob_rows = (exp_rows / totals).astype(BF)
        block_out = jnp.einsum("hqk,khd->qhd", prob_rows, values_all, preferred_element_type=F32)
        return (
            block_out.astype(BF).reshape(block_size, col_count),
            (row_max + jnp.log(totals))[..., 0],
        )

    outputs, log_totals = lax.map(
        one_block,
        (
            query_heads.reshape(block_count, block_size, head_count, HD),
            segment_all.reshape(block_count, block_size),
        ),
    )
    return outputs.reshape(total_rows, col_count), log_totals


def attend_back(query_heads, key_heads, value_heads, grad_heads, log_totals, segment_all):
    total_rows, col_count = query_heads.shape
    head_count = col_count // HD
    block_size = block_rows()
    block_count = total_rows // block_size
    keys_all = key_heads.reshape(total_rows, head_count, HD)
    values_all = value_heads.reshape(total_rows, head_count, HD)
    score_scale = HD ** (-0.5)

    def one_block(carried, pieces):
        key_sum, value_sum = carried
        query_block, grad_block, log_block, segment_block = pieces
        masked = head_scores(query_block, keys_all, segment_block, segment_all, score_scale)
        prob_rows = jnp.exp(masked - log_block[:, :, None])
        grad_probs = jnp.einsum("qhd,khd->hqk", grad_block, values_all, preferred_element_type=F32)
        inner_sum = jnp.sum(prob_rows * grad_probs, axis=-1, keepdims=True)
        grad_scores = (prob_rows * (grad_probs - inner_sum)).astype(BF)
        grad_query = (
            jnp.einsum("hqk,khd->qhd", grad_scores, keys_all, preferred_element_type=F32)
            * score_scale
        )
        key_sum = (
            key_sum
            + jnp.einsum("hqk,qhd->khd", grad_scores, query_block, preferred_element_type=F32)
            * score_scale
        )
        value_sum = value_sum + jnp.einsum(
            "hqk,qhd->khd", prob_rows.astype(BF), grad_block, preferred_element_type=F32
        )
        return (key_sum, value_sum), grad_query.astype(BF).reshape(block_size, col_count)

    zero_sums = jnp.zeros((total_rows, head_count, HD), F32)
    (key_sum, value_sum), query_grads = lax.scan(
        one_block,
        (zero_sums, zero_sums),
        (
            query_heads.reshape(block_count, block_size, head_count, HD),
            grad_heads.reshape(block_count, block_size, head_count, HD),
            log_totals,
            segment_all.reshape(block_count, block_size),
        ),
    )
    return (
        query_grads.reshape(total_rows, col_count),
        key_sum.astype(BF).reshape(total_rows, col_count),
        value_sum.astype(BF).reshape(total_rows, col_count),
    )


def own_time_features(times, first_col, col_count, model_width):
    half_width = model_width // 2
    cols = first_col + jnp.arange(col_count, dtype=jnp.int32)
    is_sine = cols < half_width
    steps_row = jnp.where(is_sine, cols, cols - half_width).astype(F32)
    frequency = jnp.exp(steps_row * (-math.log(10000.0) / (half_width - 1)))
    phase_arg = 1000.0 * times[:, None] * frequency[None, :]
    features = jnp.where(is_sine[None, :], jnp.sin(phase_arg), jnp.cos(phase_arg))
    return jax.nn.silu(features).astype(BF)


def pad_rows(vector):
    rows = -(-vector.shape[-1] // LANES)
    return jnp.pad(vector, (0, rows * LANES - vector.shape[-1])).reshape(rows, LANES)


def body(
    frames,
    skip_frames,
    lengths,
    flow_time,
    skip_weight,
    adaln_weight,
    adaln_bias,
    qkv_weight,
    qkv_bias,
    output_weight,
    output_bias,
    up_weight,
    up_bias,
    down_weight,
    down_bias,
    out_grad,
):
    n_u, n_s = lax.axis_size("utt"), lax.axis_size("sp")
    u, s = lax.axis_index("utt"), lax.axis_index("sp")
    n_all = n_u * n_s
    me = u * n_s + s
    rows, width = frames.shape
    per_group = lengths.shape[1]
    ff = up_weight.shape[1]
    part_width = width // n_s
    part_ff = ff // n_s
    lengths_row = lengths[0]

    own_ids = s * rows + jnp.arange(rows, dtype=jnp.int32)
    inside, segment_own, _ = utterance_layout(lengths_row, own_ids)
    all_ids = jnp.concatenate(
        [(s ^ d) * rows + jnp.arange(rows, dtype=jnp.int32) for d in range(n_s)]
    )
    _, segment_all, position_all = utterance_layout(lengths_row, all_ids)

    skip_lines = gather_utt(skip_weight)
    skip_parts = in_device_order(gather_sp(skip_lines))
    full_skip = jnp.stack(skip_parts, axis=1).reshape(-1, width)

    cols = qkv_weight.shape[0]
    qkv_split = qkv_weight.reshape(cols, 3, n_s, part_width).transpose(2, 0, 1, 3)
    up_split = up_weight.reshape(cols, n_u, n_s, ff // n_all).transpose(2, 0, 1, 3)
    both_split = jnp.concatenate(
        [qkv_split.reshape(n_s, cols, 3 * part_width), up_split.reshape(n_s, cols, part_ff)], axis=2
    )
    both_mine = lax.all_to_all(both_split, "sp", 0, 0, tiled=True).reshape(n_s * cols, -1)
    my_qkv = lax.all_gather(both_mine[:, : 3 * part_width], "utt", axis=0, tiled=True)
    out_lines = gather_utt(output_weight)
    out_parts = in_device_order(gather_sp(out_lines))
    full_output = jnp.stack(out_parts, axis=1).reshape(-1, width)
    ff_bundle = jnp.concatenate([both_mine[:, 3 * part_width :], down_weight], axis=0)
    ff_lines = lax.all_gather(ff_bundle, "utt", axis=0)
    my_up = ff_lines[:, : n_s * cols].reshape(width, part_ff)
    my_down = ff_lines[:, n_s * cols :].reshape(part_ff, width)

    flow_row = jnp.pad(flow_time, ((0, 0), (0, LANES - per_group)))
    flow_tiled = jnp.broadcast_to(flow_row[None], (n_u, 1, LANES))
    all_flow = lax.all_to_all(flow_tiled, "utt", 0, 0, tiled=True)
    times = all_flow[:, 0, :per_group].reshape(n_u * per_group)
    feature_rows = adaln_weight.shape[0]
    silu_own = own_time_features(times, me * feature_rows, feature_rows, width)
    table_width = adaln_weight.shape[1]
    mod_terms = dot32(silu_own, adaln_weight)
    bias_row = lax.dynamic_update_slice(
        jnp.zeros((table_width,), F32), adaln_bias.astype(F32), (me * adaln_bias.shape[0],)
    )
    mod_terms = mod_terms + bias_row[None, :]
    table_rows = per_group * table_width // LANES
    bias_sizes = [qkv_bias.shape[0], output_bias.shape[0], up_bias.shape[0], down_bias.shape[0]]
    bias_own = pad_rows(
        jnp.concatenate([qkv_bias, output_bias, up_bias, down_bias]).astype(F32)
    )
    bias_rows = bias_own.shape[0]
    small = jnp.concatenate(
        [
            mod_terms.reshape(n_u, table_rows, LANES),
            jnp.broadcast_to(bias_own[None], (n_u, bias_rows, LANES)),
        ],
        axis=1,
    )
    small = lax.all_to_all(small, "utt", 0, 0, tiled=True)
    mod_part = jnp.sum(small[:, :table_rows], axis=0)
    bias_part = small[:, table_rows:].reshape(n_u * bias_rows, LANES)
    slots = jnp.where((jnp.arange(n_s) == s)[:, None, None], bias_part[None], 0.0)
    message = jnp.concatenate([mod_part, slots.reshape(-1, LANES)], axis=0)
    message = sum_sp(message)
    mod_table = message[:table_rows].reshape(per_group, table_width)
    bias_all = message[table_rows:].reshape(n_s, n_u, bias_rows * LANES).transpose(1, 0, 2)
    offsets = [0]
    for size in bias_sizes:
        offsets.append(offsets[-1] + size)
    full_qkv_bias, full_output_bias, full_up_bias, full_down_bias = [
        bias_all[:, :, offsets[i] : offsets[i + 1]].reshape(-1) for i in range(4)
    ]
    my_qkv_bias = lax.dynamic_slice_in_dim(
        full_qkv_bias.reshape(3, width), s * part_width, part_width, 1
    ).reshape(-1)
    my_up_bias = lax.dynamic_index_in_dim(
        full_up_bias.reshape(n_u, n_s, -1), s, 1, keepdims=False
    ).reshape(-1)

    def expand(block):
        table = mod_table[:, block * width : (block + 1) * width]
        result = table[per_group - 1][None, :]
        for k in range(per_group - 2, -1, -1):
            result = jnp.where(segment_own[:, None] == k, table[k][None, :], result)
        return result

    def segment_sums(values):
        return jnp.stack(
            [jnp.sum(jnp.where(inside[:, k][:, None], values, 0.0), axis=0) for k in range(per_group)]
        )

    shift_attn, scale_attn, gate_attn, shift_ffn, scale_ffn, gate_ffn = [expand(i) for i in range(6)]

    grad_out = out_grad.astype(F32)
    grad_result = (gate_ffn * grad_out).astype(BF)
    grad_result_all = jnp.concatenate(gather_sp(grad_result), axis=0)

    base_rows = dot32(frames, full_skip[:width]) + dot32(skip_frames, full_skip[width:])
    base_norm, base_scale = norm_parts(base_rows)
    normed = (base_norm * (1.0 + scale_attn) + shift_attn).astype(BF)
    normed_all = jnp.concatenate(gather_sp(normed), axis=0)
    projected = dot32(normed_all, my_qkv) + my_qkv_bias[None, :]
    query_rows = rotary(projected[:, :part_width], position_all, 1.0).astype(BF)
    key_rows = rotary(projected[:, part_width : 2 * part_width], position_all, 1.0).astype(BF)
    value_rows = projected[:, 2 * part_width :].astype(BF)
    attended_heads, log_totals = attend(query_rows, key_rows, value_rows, segment_all)
    arrived = exchange_sp([attended_heads[d * rows : (d + 1) * rows] for d in range(n_s)])
    attended = jnp.concatenate(in_device_order(arrived), axis=1)
    branch = dot32(attended, full_output) + full_output_bias[None, :]
    middle = base_rows + gate_attn * branch
    middle_norm, middle_scale = norm_parts(middle)
    normed_ffn = (middle_norm * (1.0 + scale_ffn) + shift_ffn).astype(BF)
    normed_ffn_all = jnp.concatenate(gather_sp(normed_ffn), axis=0)
    hidden = dot32(normed_ffn_all, my_up) + my_up_bias[None, :]
    active_wide, gelu_pull = jax.vjp(gelu_tanh, hidden)
    active = active_wide.astype(BF)

    grad_active = dot_nt(grad_result_all, my_down)
    grad_hidden = gelu_pull(grad_active)[0].astype(BF)
    grad_nffn_part = dot_nt(grad_hidden, my_up)
    grad_normed_ffn = reduce_sp([grad_nffn_part[d * rows : (d + 1) * rows] for d in range(n_s)])

    result_part = dot32(active, my_down)
    result = reduce_sp([result_part[d * rows : (d + 1) * rows] for d in range(n_s)])
    result = result + full_down_bias[None, :]
    mixed_out = (middle + gate_ffn * result).astype(BF)
    grad_gate_ffn = grad_out * result

    grad_down = dot_tn(active, grad_result_all)
    grad_up = dot_tn(normed_ffn_all, grad_hidden)
    grad_up_bias = jnp.sum(grad_hidden.astype(F32), axis=0)
    grad_down_bias = jnp.sum(grad_result.astype(F32), axis=0)
    down_sum = lax.psum_scatter(
        grad_down.astype(BF), "utt", scatter_dimension=0, tiled=True
    ).astype(F32)
    up_mine = lax.psum_scatter(grad_up.astype(BF), "utt", scatter_dimension=0, tiled=True)
    up_back = lax.all_to_all(up_mine.reshape(n_s, cols, part_ff), "sp", 0, 0, tiled=True)
    up_sum = (
        up_back.reshape(n_s, cols, n_u, ff // n_all).transpose(1, 2, 0, 3).reshape(cols, ff)
    ).astype(F32)

    grad_scale_ffn = grad_normed_ffn * middle_norm
    grad_middle = grad_out + norm_back(
        middle_norm, middle_scale, grad_normed_ffn * (1.0 + scale_ffn)
    )
    grad_gate_attn = grad_middle * branch
    grad_branch = (gate_attn * grad_middle).astype(BF)
    grad_output_bias = jnp.sum(grad_branch.astype(F32), axis=0)
    grad_branch_all = jnp.concatenate(gather_sp(grad_branch), axis=0)
    my_output = lax.dynamic_slice_in_dim(full_output, s * part_width, part_width, 0)
    grad_heads = dot_nt(grad_branch_all, my_output).astype(BF)
    grad_output = dot_tn(attended_heads, grad_branch_all)
    out_sum = to_owner(scatter_utt(grad_output.reshape(n_u, -1, width)).astype(F32))

    grad_query, grad_key, grad_value = attend_back(
        query_rows, key_rows, value_rows, grad_heads, log_totals, segment_all
    )
    grad_projected = jnp.concatenate(
        [
            rotary(grad_query.astype(F32), position_all, -1.0).astype(BF),
            rotary(grad_key.astype(F32), position_all, -1.0).astype(BF),
            grad_value,
        ],
        axis=1,
    )
    grad_normed_part = dot_nt(grad_projected, my_qkv)
    grad_normed = reduce_sp([grad_normed_part[d * rows : (d + 1) * rows] for d in range(n_s)])
    grad_qkv = dot_tn(normed_all, grad_projected)
    my_qkv_bias_grad = jnp.sum(grad_projected.astype(F32), axis=0)
    qkv_mine = scatter_utt(grad_qkv.reshape(n_u, n_s * cols, 3 * part_width))
    qkv_back = lax.all_to_all(
        qkv_mine.astype(BF).reshape(n_s, cols, 3 * part_width), "sp", 0, 0, tiled=True
    )
    qkv_sum = (
        qkv_back.reshape(n_s, cols, 3, part_width).transpose(1, 2, 0, 3).reshape(cols, 3 * width)
    ).astype(F32)

    grad_scale_attn = grad_normed * base_norm
    grad_base = (
        grad_middle + norm_back(base_norm, base_scale, grad_normed * (1.0 + scale_attn))
    ).astype(BF)
    grad_base_all = jnp.concatenate(gather_sp(grad_base), axis=0)
    part_joined = 2 * width // n_s
    joined = jnp.concatenate([frames, skip_frames], axis=1)
    joined_mine = jnp.concatenate(
        exchange_sp(
            [
                lax.dynamic_slice_in_dim(joined, (s ^ d) * part_joined, part_joined, 1)
                for d in range(n_s)
            ]
        ),
        axis=0,
    )
    grad_skip = dot_tn(joined_mine, grad_base_all)
    skip_sum = to_owner(scatter_utt(grad_skip.reshape(n_u, -1, width)).astype(F32))
    frames_grad = dot_nt(grad_base, full_skip[:width])
    skip_grad = dot_nt(grad_base, full_skip[width:])

    grad_table = jnp.concatenate(
        [
            segment_sums(v)
            for v in (
                grad_normed,
                grad_scale_attn,
                grad_gate_attn,
                grad_normed_ffn,
                grad_scale_ffn,
                grad_gate_ffn,
            )
        ],
        axis=1,
    )
    qkv_bias_slots = lax.dynamic_update_slice(
        jnp.zeros((3, width), F32), my_qkv_bias_grad.reshape(3, part_width), (0, s * part_width)
    ).reshape(-1)
    up_bias_slots = lax.dynamic_update_slice(
        jnp.zeros((n_u, n_s, ff // n_all), F32),
        grad_up_bias.reshape(n_u, 1, ff // n_all),
        (0, s, 0),
    ).reshape(-1)
    bias_vec = jnp.concatenate(
        [
            v.reshape(n_u, -1)
            for v in (qkv_bias_slots, grad_output_bias, up_bias_slots, grad_down_bias)
        ],
        axis=1,
    )
    vec_rows = -(-bias_vec.shape[1] // LANES)
    bias_vec = jnp.pad(bias_vec, ((0, 0), (0, vec_rows * LANES - bias_vec.shape[1])))
    tail = jnp.concatenate(
        [grad_table.reshape(table_rows, LANES), bias_vec.reshape(n_u * vec_rows, LANES)], axis=0
    )
    tail = sum_sp(tail)
    tail = jnp.concatenate(
        [
            jnp.broadcast_to(tail[None, :table_rows], (n_u, table_rows, LANES)),
            tail[table_rows:].reshape(n_u, vec_rows, LANES),
        ],
        axis=1,
    )
    tail = lax.all_to_all(tail, "utt", 0, 0, tiled=True)
    table_all = tail[:, :table_rows].reshape(n_u * per_group, table_width)
    adaln_sum = lax.dot_general(
        silu_own.astype(F32),
        table_all,
        (((0,), (0,)), ((), ())),
        precision=highest_precision,
        preferred_element_type=F32,
    )
    adaln_bias_sum = jnp.sum(owned(table_all), axis=0)
    vec = jnp.sum(tail[:, table_rows:], axis=0).reshape(-1)
    bias_sums, start = [], 0
    for size in bias_sizes:
        bias_sums.append(lax.dynamic_slice_in_dim(vec, start + s * size, size, 0))
        start += size * n_s

    return (
        mixed_out,
        frames_grad,
        skip_grad,
        skip_sum,
        adaln_sum,
        adaln_bias_sum,
        qkv_sum,
        bias_sums[0],
        out_sum,
        bias_sums[1],
        up_sum,
        bias_sums[2],
        down_sum,
        bias_sums[3],
    )


def solution(mesh):
    both = ("utt", "sp")
    matrix, vector, group = P(both, None), P(both), P("utt", None)
    return jax.shard_map(
        body,
        mesh=mesh,
        in_specs=(
            matrix,
            matrix,
            group,
            group,
            matrix,
            matrix,
            vector,
            matrix,
            vector,
            matrix,
            vector,
            matrix,
            vector,
            matrix,
            vector,
            matrix,
        ),
        out_specs=(
            matrix,
            matrix,
            matrix,
            matrix,
            matrix,
            vector,
            matrix,
            vector,
            matrix,
            vector,
            matrix,
            vector,
            matrix,
            vector,
        ),
        check_vma=False,
    )
```

time: 1600 us -> 493 us (0.31)
  waiting for transfers between devices: 1150 us -> 170 us
  blocking collectives: 129 us -> 0 us
  matrix products: 155 us -> 103 us
  starting transfers between devices: 30 us -> 74.8 us
  other arithmetic: 35.7 us -> 69.3 us
  local copies, waits for them, and re-layouts: 69.7 us -> 48.9 us
    reduce_scatter x6 -> x2, waiting for transfers between devices: 854 us -> 0.01 us  [the longest x1 0.01 us: body(): lax.psum_scatter(grad_up.astype(BF), 'utt', scatter_dimension=0, tiled=True)]
    all_gather x6 -> x2, waiting for transfers between devices: 238 us -> 8.05 us  [the longest x1 8.05 us: body(): ff_lines = lax.all_gather(ff_bundle, 'utt', axis=0)]
    ppermute x0 -> x47, waiting for transfers between devices: none -> 94.5 us  [the longest x40 59.6 us: xor_sp(): return lax.ppermute(values, 'sp', [(i, i ^ distance) for i in range(size)])]
    unnamed x2 -> x0, blocking collectives: 85.4 us -> none
    dot_general x21, matrix products: 128 us -> 70.3 us  [the longest x6 24.2 us: dot_nt(): lax.dot_general(left, right, (((1,), (1,)), ((), ())), preferred_element_...]
    all_gather x1 -> x0, blocking collectives: 43.3 us -> none  [body(): lax.all_gather(up_bias, ('utt', 'sp'), axis=0, tiled=True)]
    ppermute x0 -> x47, starting transfers between devices: none -> 27.8 us  [the longest x40 20.1 us: xor_sp(): return lax.ppermute(values, 'sp', [(i, i ^ distance) for i in range(size)])]
    all_to_all x8 -> x11, starting transfers between devices: 28.9 us -> 46.7 us  [the longest x3 12.8 us: scatter_utt(): lax.all_to_all(half, 'utt', 0, 0, axis_index_groups=high_groups(), tiled=...]
  transfers between devices with their start and end apart: 20 -> 62, of which waited for: 17 -> 26; matrix products, arithmetic and copies ran while one was open for 13% -> 41% of each run, Pallas kernels for 0% -> 0%
where the time goes in v1:
time: 493 us; the launch traced here: 483 us
  waiting for transfers between devices  170 us (34%)
  matrix products  103 us (21%)
  starting transfers between devices  74.8 us (15%)
  other arithmetic  69.3 us (14%)
  local copies, waits for them, and re-layouts  48.9 us (10%)
  between operations  16.6 us (3%)
    ppermute x40, waiting for transfers between devices, xor_sp(): return lax.ppermute(values, 'sp', [(i, i ^ distance) for i in range(size)])  59.6 us
    ppermute x3, waiting for transfers between devices, scatter_utt(): arrived = lax.ppermute(send.astype(BF), 'utt', low_partner())  27.1 us
    dot_general x6, matrix products, dot_nt(): lax.dot_general(left, right, (((1,), (1,)), ((), ())), preferred_element_...  24.2 us
    ppermute x40, starting transfers between devices, xor_sp(): return lax.ppermute(values, 'sp', [(i, i ^ distance) for i in range(size)])  20.1 us
    dot_general x5, matrix products, dot_tn(): lax.dot_general(left, right, (((0,), (0,)), ((), ())), preferred_element_...  19.4 us
    all_to_all x2, waiting for transfers between devices, gather_utt(): lax.all_to_all(tiled, 'utt', 0, 0, axis_index_groups=high_groups(), tiled...  18.1 us
    dot_general x7, matrix products, dot32(): return jnp.dot(left, right, preferred_element_type=F32)  17 us
    all_to_all x3, waiting for transfers between devices, scatter_utt(): lax.all_to_all(half, 'utt', 0, 0, axis_index_groups=high_groups(), tiled=...  13.9 us
  transfers between devices with their start and end apart: 62, of which 26 were waited for; matrix products, arithmetic and copies ran while one was open for 41% of the time, Pallas kernels for 0%

profile of v1, /device:TPU:4, one launch (start us, length us, event | category | flops | bytes accessed | tf_op | source)
XLA Modules:
  0.0 483.4 jit_solution(10293891380672507654)
XLA Ops:
  9.1 4.9 %all-to-all-start = ((bf16[4,64,1024]{2,1,0:T(8,128)(2,1)}), bf16[4,64,1024]{2,1,0:T(8,128)(2,1)S(1)}, u32[]{:S(2)}, u32[]{:S(2)}) async-start(bf16[4,64,1024]{2,1,0:T(8,128)(2,1)} %broadcast_in_dim.491), calls=%async_computation | async-start | bytes 1048576 | tf_op jit(solution)/shard_map/all_to_all | solution.py:93
  18.7 9.7 %all-to-all-done = bf16[4,64,1024]{2,1,0:T(8,128)(2,1)S(1)} async-done(((bf16[4,64,1024]{2,1,0:T(8,128)(2,1)}), bf16[4,64,1024]{2,1,0:T(8,128)(2,1)S(1)}, u32[]{:S(2)}, u32[]{:S(2)}) %all-to-all-start) | async-done | bytes 524320 | tf_op jit(solution)/shard_map/all_to_all | solution.py:93
  33.3 4.9 %all-to-all-done.1 = f32[8,1,128]{2,1,0:T(1,128)S(1)} async-done(((f32[8,1,128]{2,1,0:T(1,128)}), f32[8,1,128]{2,1,0:T(1,128)S(1)}, u32[]{:S(2)}, u32[]{:S(2)}) %all-to-all-start.1) | async-done | bytes 4128 | tf_op jit(solution)/shard_map/all_to_all | solution.py:342
  43.6 6.1 %all-to-all-done.3 = bf16[4,32,1792]{2,1,0:T(8,128)(2,1)S(1)} async-done(((bf16[4,32,1792]{2,1,0:T(8,128)(2,1)}), bf16[4,32,1792]{2,1,0:T(8,128)(2,1)S(1)}, u32[]{:S(2)}, u32[]{:S(2)}) %all-to-all-start.3) | async-done | bytes 458784 | tf_op jit(solution)/shard_map/all_to_all | solution.py:330
  54.5 8.3 %all-to-all-done.4 = bf16[4,32,1024]{2,1,0:T(8,128)(2,1)S(1)} async-done(((bf16[4,32,1024]{2,1,0:T(8,128)(2,1)}), bf16[4,32,1024]{2,1,0:T(8,128)(2,1)S(1)}, u32[]{:S(2)}, u32[]{:S(2)}) %all-to-all-start.4) | async-done | bytes 262176 | tf_op jit(solution)/shard_map/all_to_all | solution.py:93
  62.9 4.9 %all-to-all-start.2 = ((f32[8,147,128]{2,1,0:T(8,128)}), f32[8,147,128]{2,1,0:T(8,128)S(1)}, u32[]{:S(2)}, u32[]{:S(2)}) async-start(f32[8,147,128]{2,1,0:T(8,128)} %pad_maximum_fusion.11), calls=%async_computation.2 | async-start | bytes 1245184 | tf_op jit(solution)/shard_map/all_to_all | solution.py:365
  70.5 12.0 %all-to-all-done.2 = f32[8,147,128]{2,1,0:T(8,128)S(1)} async-done(((f32[8,147,128]{2,1,0:T(8,128)}), f32[8,147,128]{2,1,0:T(8,128)S(1)}, u32[]{:S(2)}, u32[]{:S(2)}) %all-to-all-start.2) | async-done | bytes 602144 | tf_op jit(solution)/shard_map/all_to_all | solution.py:365
  83.8 4.8 collective-permute-done.4
  106.5 8.0 %collective-permute-done.7 = bf16[256,1024]{1,0:T(8,128)(2,1)} collective-permute-done((bf16[256,1024]{1,0:T(8,128)(2,1)S(1)}, bf16[256,1024]{1,0:T(8,128)(2,1)}, u32[]{:S(2)}, u32[]{:S(2)}) %collective-permute-start.7) | collective-permute-done | bytes 524320 | tf_op jit(solution)/shard_map/ppermute | solution.py:30
  124.2 16.5 %while.27 = (s32[]{:T(128)}, bf16[2,512,256]{2,1,0:T(8,128)(2,1)}, f32[2,4,512]{2,1,0:T(4,128)S(1)}, s32[2,512]{1,0:T(2,128)S(1)}, s32[1024]{0:T(1024)S(1)}, /*i...) while((s32[]{:T(128)}, bf16[2,512,256]{2,1,0:T(8,128)(2,1)}, ...), condition=%wide.region_10.11_spmd, body=%wide.region_7.10_spmd.sunk | while | flops 562690048 | bytes 29960808 | solution.py:209
  156.8 12.9 %collective-permute-done.17 = bf16[256,1024]{1,0:T(8,128)(2,1)} collective-permute-done((bf16[256,1024]{1,0:T(8,128)(2,1)}, bf16[256,1024]{1,0:T(8,128)(2,1)}, u32[]{:S(2)}, u32[]{:S(2)}) %collective-permute-start.17) | collective-permute-done | bytes 524320 | tf_op jit(solution)/shard_map/ppermute | solution.py:30
  170.3 10.4 %collective-permute-done.23 = bf16[256,1024]{1,0:T(8,128)(2,1)} collective-permute-done((bf16[256,1024]{1,0:T(8,128)(2,1)}, bf16[256,1024]{1,0:T(8,128)(2,1)}, u32[]{:S(2)}, u32[]{:S(2)}) %collective-permute-start.23) | collective-permute-done | bytes 524320 | tf_op jit(solution)/shard_map/ppermute | solution.py:30
  180.7 8.1 %all-gather.6.cloned.1.call-done = bf16[2048,1024]{1,0:T(8,128)(2,1)} async-done(((bf16[256,1024]{1,0:T(8,128)(2,1)}), bf16[2048,1024]{1,0:T(8,128)(2,1)}) %all-gather.6.cloned.1.call-update) | async-done | bytes 4194320 | tf_op jit(solution)/shard_map/all_gather | solution.py:336
  191.5 4.6 fusion.100
  196.1 8.4 %convert_reduce_fusion = (f32[1024]{0:T(1024)S(1)}, bf16[1024,1024]{1,0:T(8,128)(2,1)S(1)}) fusion(f32[1024,1024]{1,0:T(8,128)S(1)} %fusion.100, f32[1024]{0:T(1024)S(1)} %fusion.117, bf16[1024,1024]{1,0:T(8,128)(2,1)S(1)} %bitcast.359, bf16[256,1024]{1,0:T(8,128)(2,1)} %collective-permute-done.24, bf16[256,1024]{1,0:T(8,128)(2,1)} %collective-permute-done.23, ...), kind=kOutput, calls=%fused_computation.62 | convolution fusion | flops 2179988480 | bytes 10493952 | tf_op jit(solution)/shard_map/dot_general | solution.py:21
  204.5 4.4 fusion.167
  209.9 5.3 %convolution_convert_fusion.1 = bf16[1024,1024]{1,0:T(8,128)(2,1)} fusion(bf16[1024,1024]{1,0:T(8,128)(2,1)S(1)} %get-tuple-element.464, bf16[256,1024]{1,0:T(8,128)(2,1)} %collective-permute-done.18, bf16[256,1024]{1,0:T(8,128)(2,1)} %collective-permute-done.17, bf16[256,1024]{1,0:T(8,128)(2,1)} %collective-permute-done.16, ...), kind=kOutput, calls=%fused_computation.86 | convolution fusion | flops 2156920832 | bytes 6291456 | tf_op jit(solution)/shard_map/dot_general | solution.py:25
  225.2 7.2 %collective-permute-done.27 = bf16[256,1024]{1,0:T(8,128)(2,1)} collective-permute-done((bf16[256,1024]{1,0:T(8,128)(2,1)}, bf16[256,1024]{1,0:T(8,128)(2,1)}, u32[]{:S(2)}, u32[]{:S(2)}) %collective-permute-start.27) | collective-permute-done | bytes 524320 | tf_op jit(solution)/shard_map/ppermute | solution.py:30
  241.0 4.9 %fusion.169 = (bf16[1024,1024]{1,0:T(8,128)(2,1)S(1)}, f32[1024,1024]{1,0:T(8,128)}) fusion(bf16[1024,1024]{1,0:T(8,128)(2,1)S(1)} %bitcast.360, f32[1024,1024]{1,0:T(8,128)S(1)} %copy-done.118, f32[1024]{0:T(1024)S(1)} %fusion.117), kind=kOutput, calls=%fused_computation.354 | convolution fusion | flops 2159017984 | bytes 12587008 | tf_op jit(solution)/shard_map/dot_general | solution.py:17
  247.3 5.6 %collective-permute-done.29 = bf16[256,1024]{1,0:T(8,128)(2,1)} collective-permute-done((bf16[256,1024]{1,0:T(8,128)(2,1)}, bf16[256,1024]{1,0:T(8,128)(2,1)}, u32[]{:S(2)}, u32[]{:S(2)}) %collective-permute-start.29) | collective-permute-done | bytes 524320 | tf_op jit(solution)/shard_map/ppermute | solution.py:30
  252.9 6.0 %convolution_convert_fusion = bf16[1024,1024]{1,0:T(8,128)(2,1)} fusion(bf16[256,1024]{1,0:T(8,128)(2,1)} %collective-permute-done.24, bf16[256,1024]{1,0:T(8,128)(2,1)} %collective-permute-done.23, bf16[256,1024]{1,0:T(8,128)(2,1)} %collective-permute-done.22, bf16[256,1024]{1,0:T(8,128)(2,1)} %get-tuple-element.356, f32[1024,1024]{1,0:T(8,128)S(1)} %copy-done.118, ...), kind=kOutput, calls=%fused_computation.85 | convolution fusion | flops 2167406592 | bytes 8392704 | tf_op jit(solution)/shard_map/dot_general | solution.py:25
  267.3 42.6 %while.28 = (s32[]{:T(128)}, f32[1024,4,64]{0,2,1:T(8,128)S(1)}, f32[1024,4,64]{0,2,1:T(8,128)}, bf16[2,512,256]{1,2,0:T(8,128)(2,1)}, bf16[2,512,4,64]{1,3,2,0:...) while((s32[]{:T(128)}, f32[1024,4,64]{0,2,1:T(8,128)S(1)}, ...), condition=%wide.region_17.18_spmd.clone, body=%wide.region_15.17_spmd.clone.sunk | while | flops 1375729664 | bytes 148179280 | solution.py:251
  279.5 4.2 fusion.235
  305.1 4.6 fusion.234
  337.4 13.4 %collective-permute-done.44 = bf16[4,128,768]{2,1,0:T(8,128)(2,1)S(1)} collective-permute-done((bf16[4,128,768]{2,1,0:T(8,128)(2,1)S(1)}, bf16[4,128,768]{2,1,0:T(8,128)(2,1)S(1)}, u32[]{:S(2)}, u32[]{:S(2)}) %collective-permute-start.44) | collective-permute-done | bytes 786464 | tf_op jit(solution)/shard_map/ppermute | solution.py:109
  353.4 4.4 all-to-all-start.7
  367.1 10.8 %all-to-all-done.7 = bf16[4,128,768]{2,1,0:T(8,128)(2,1)} async-done(((bf16[4,128,768]{2,1,0:T(8,128)(2,1)}), bf16[4,128,768]{2,1,0:T(8,128)(2,1)}, u32[]{:S(2)}, u32[]{:S(2)}) %all-to-all-start.7) | async-done | bytes 786464 | tf_op jit(solution)/shard_map/all_to_all | solution.py:111
  403.2 9.2 %all-to-all-done.10 = bf16[4,32,1024]{2,1,0:T(8,128)(2,1)S(1)} async-done(((bf16[4,32,1024]{2,1,0:T(8,128)(2,1)}), bf16[4,32,1024]{2,1,0:T(8,128)(2,1)S(1)}, u32[]{:S(2)}, u32[]{:S(2)}) %all-to-all-start.10) | async-done | bytes 262176 | tf_op jit(solution)/shard_map/all_to_all | solution.py:443
  412.3 6.2 %all-to-all-start.6 = ((f32[8,153,128]{2,1,0:T(8,128)}), f32[8,153,128]{2,1,0:T(8,128)}, u32[]{:S(2)}, u32[]{:S(2)}) async-start(f32[8,153,128]{2,1,0:T(8,128)} %pad_maximum_fusion.10), calls=%async_computation.6 | async-start | bytes 1310720 | tf_op jit(solution)/shard_map/all_to_all | solution.py:547
  423.8 13.7 %collective-permute-done.40 = bf16[4,64,1024]{2,1,0:T(8,128)(2,1)S(1)} collective-permute-done((bf16[4,64,1024]{2,1,0:T(8,128)(2,1)S(1)}, bf16[4,64,1024]{2,1,0:T(8,128)(2,1)S(1)}, u32[]{:S(2)}, u32[]{:S(2)}) %collective-permute-start.40) | collective-permute-done | bytes 524320 | tf_op jit(solution)/shard_map/ppermute | solution.py:109
  439.0 5.0 %all-to-all-start.5 = ((bf16[4,64,1024]{2,1,0:T(8,128)(2,1)}), bf16[4,64,1024]{2,1,0:T(8,128)(2,1)S(1)}, u32[]{:S(2)}, u32[]{:S(2)}) async-start(bf16[4,64,1024]{2,1,0:T(8,128)(2,1)} %fusion.80), calls=%async_computation.5 | async-start | bytes 1048576 | tf_op jit(solution)/shard_map/all_to_all | solution.py:111
  466.4 7.8 %collective-permute-done.41 = f32[64,1024]{1,0:T(8,128)S(1)} collective-permute-done((f32[64,1024]{1,0:T(8,128)S(1)}, f32[64,1024]{1,0:T(8,128)S(1)}, u32[]{:S(2)}, u32[]{:S(2)}) %collective-permute-start.41) | collective-permute-done | bytes 262176 | tf_op jit(solution)/shard_map/ppermute | solution.py:121
  (588 shorter events, 245.5 us)
Async XLA Ops:
  9.1 19.4 %all-to-all-start = ((bf16[4,64,1024]{2,1,0:T(8,128)(2,1)}), bf16[4,64,1024]{2,1,0:T(8,128)(2,1)S(1)}, u32[]{:S(2)}, u32[]{:S(2)}) async-start(bf16[4,64,1024]{2,1,0:T(8,128)(2,1)} %broadcast_in_dim.491), calls=%async_computation | async-start | bytes 1048576 | tf_op jit(solution)/shard_map/all_to_all | solution.py:93
  33.3 20.7 %collective-permute-start = (bf16[4,64,1024]{2,1,0:T(8,128)(2,1)S(1)}, bf16[4,64,1024]{2,1,0:T(8,128)(2,1)S(1)}, u32[]{:S(2)}, u32[]{:S(2)}) collective-permute-start(bf16[4,64,1024]{2,1,0:T(8,128)(2,1)S(1)} %all-to-all-done), channel_id=1, source_target_pairs={{0,4},{4,0},{8,12},{12,8},{16,20},{20,16},{24,28},{28,24},{1,5},{5... | collective-permute-start | bytes 1572872 | tf_op jit(solution)/shard_map/ppermute | solution.py:96
  54.1 28.6 %collective-permute-start.2 = (bf16[8,64,1024]{2,1,0:T(8,128)(2,1)S(1)}, bf16[8,64,1024]{2,1,0:T(8,128)(2,1)}, u32[]{:S(2)}, u32[]{:S(2)}) collective-permute-start(bf16[8,64,1024]{2,1,0:T(8,128)(2,1)S(1)} %bitcast.346), channel_id=1, source_target_pairs={{0,2},{1,3},{2,0},{3,1},{4,6},{5,7},{6,4},{7,5},{8,10},{9,11},{10,... | collective-permute-start | bytes 3145736 | tf_op jit(solution)/shard_map/ppermute | solution.py:30
  62.9 19.6 %all-to-all-start.2 = ((f32[8,147,128]{2,1,0:T(8,128)}), f32[8,147,128]{2,1,0:T(8,128)S(1)}, u32[]{:S(2)}, u32[]{:S(2)}) async-start(f32[8,147,128]{2,1,0:T(8,128)} %pad_maximum_fusion.11), calls=%async_computation.2 | async-start | bytes 1245184 | tf_op jit(solution)/shard_map/all_to_all | solution.py:365
  67.8 50.3 %all-gather.4.cloned.1.call-start = ((), (), s32[]{:S(2)}) async-start(), calls=%async_computation.13 | async-start | bytes 1769472 | tf_op jit(solution)/shard_map/all_gather | solution.py:331
  70.5 118.3 %all-gather.6.cloned.1.call-start = ((), (), s32[]{:S(2)}) async-start(), calls=%async_computation.16 | async-start | bytes 4718592 | tf_op jit(solution)/shard_map/all_gather | solution.py:336
  98.7 15.8 %collective-permute-start.7 = (bf16[256,1024]{1,0:T(8,128)(2,1)S(1)}, bf16[256,1024]{1,0:T(8,128)(2,1)}, u32[]{:S(2)}, u32[]{:S(2)}) collective-permute-start(bf16[256,1024]{1,0:T(8,128)(2,1)S(1)} %add_convert_fusion.3), channel_id=1, source_target_pairs={{0,2},{1,3},{2,0},{3,1},{4,6},{5,7},{6,4},{7,5},{8,10},{9,11},{10,... | collective-permute-start | bytes 1572872 | tf_op jit(solution)/shard_map/ppermute | solution.py:30
  105.5 290.9 %reduce-scatter.3.cloned.1.call-start = ((), (), s32[]{:S(2)}) async-start(), calls=%async_computation.14 | async-start | bytes 2359296 | tf_op jit(solution)/shard_map/reduce_scatter | solution.py:442
  155.1 25.6 %collective-permute-start.23 = (bf16[256,1024]{1,0:T(8,128)(2,1)}, bf16[256,1024]{1,0:T(8,128)(2,1)}, u32[]{:S(2)}, u32[]{:S(2)}) collective-permute-start(bf16[256,1024]{1,0:T(8,128)(2,1)} %get-tuple-element.356), channel_id=1, source_target_pairs={{0,2},{1,3},{2,0},{3,1},{4,6},{5,7},{6,4},{7,5},{8,10},{9,11},{10,... | collective-permute-start | bytes 1572872 | tf_op jit(solution)/shard_map/ppermute | solution.py:30
  156.6 34.8 %collective-permute-start.16 = (bf16[256,1024]{1,0:T(8,128)(2,1)}, bf16[256,1024]{1,0:T(8,128)(2,1)}, u32[]{:S(2)}, u32[]{:S(2)}) collective-permute-start(bf16[256,1024]{1,0:T(8,128)(2,1)} %get-tuple-element.451), channel_id=1, source_target_pairs={{0,1},{1,0},{2,3},{3,2},{4,5},{5,4},{6,7},{7,6},{8,9},{9,8},{10,11... | collective-permute-start | bytes 1572872 | tf_op jit(solution)/shard_map/ppermute | solution.py:30
  169.7 21.7 %collective-permute-start.18 = (bf16[256,1024]{1,0:T(8,128)(2,1)}, bf16[256,1024]{1,0:T(8,128)(2,1)}, u32[]{:S(2)}, u32[]{:S(2)}) collective-permute-start(bf16[256,1024]{1,0:T(8,128)(2,1)} %collective-permute-done.17), channel_id=1, source_target_pairs={{0,1},{1,0},{2,3},{3,2},{4,5},{5,4},{6,7},{7,6},{8,9},{9,8},{10,11... | collective-permute-start | bytes 1572872 | tf_op jit(solution)/shard_map/ppermute | solution.py:30
  169.8 26.3 %collective-permute-start.22 = (bf16[256,1024]{1,0:T(8,128)(2,1)}, bf16[256,1024]{1,0:T(8,128)(2,1)}, u32[]{:S(2)}, u32[]{:S(2)}) collective-permute-start(bf16[256,1024]{1,0:T(8,128)(2,1)} %get-tuple-element.356), channel_id=1, source_target_pairs={{0,1},{1,0},{2,3},{3,2},{4,5},{5,4},{6,7},{7,6},{8,9},{9,8},{10,11... | collective-permute-start | bytes 1572872 | tf_op jit(solution)/shard_map/ppermute | solution.py:30
  180.7 15.4 %collective-permute-start.24 = (bf16[256,1024]{1,0:T(8,128)(2,1)}, bf16[256,1024]{1,0:T(8,128)(2,1)}, u32[]{:S(2)}, u32[]{:S(2)}) collective-permute-start(bf16[256,1024]{1,0:T(8,128)(2,1)} %collective-permute-done.23), channel_id=1, source_target_pairs={{0,1},{1,0},{2,3},{3,2},{4,5},{5,4},{6,7},{7,6},{8,9},{9,8},{10,11... | collective-permute-start | bytes 1572872 | tf_op jit(solution)/shard_map/ppermute | solution.py:30
  215.3 233.9 %reduce-scatter.5.cloned.1.call-start = ((), (), s32[]{:S(2)}) async-start(), calls=%async_computation.15 | async-start | bytes 2359296 | tf_op jit(solution)/shard_map/reduce_scatter | solution.py:439
  246.8 113.0 %collective-permute-start.19 = (bf16[256,1024]{1,0:T(8,128)(2,1)}, bf16[256,1024]{1,0:T(8,128)(2,1)}, u32[]{:S(2)}, u32[]{:S(2)}) collective-permute-start(bf16[256,1024]{1,0:T(8,128)(2,1)} %get-tuple-element.386), channel_id=1, source_target_pairs={{0,1},{1,0},{2,3},{3,2},{4,5},{5,4},{6,7},{7,6},{8,9},{9,8},{10,11... | collective-permute-start | bytes 1572872 | tf_op jit(solution)/shard_map/ppermute | solution.py:30
  315.7 19.2 %collective-permute-start.45 = (bf16[4,32,1024]{2,1,0:T(8,128)(2,1)}, bf16[4,32,1024]{2,1,0:T(8,128)(2,1)}, u32[]{:S(2)}, u32[]{:S(2)}) collective-permute-start(bf16[4,32,1024]{2,1,0:T(8,128)(2,1)} %fusion.102), channel_id=1, source_target_pairs={{0,4},{4,0},{8,12},{12,8},{16,20},{20,16},{24,28},{28,24},{1,5},{5... | collective-permute-start | bytes 786440 | tf_op jit(solution)/shard_map/ppermute | solution.py:109
  328.3 22.5 %collective-permute-start.44 = (bf16[4,128,768]{2,1,0:T(8,128)(2,1)S(1)}, bf16[4,128,768]{2,1,0:T(8,128)(2,1)S(1)}, u32[]{:S(2)}, u32[]{:S(2)}) collective-permute-start(bf16[4,128,768]{2,1,0:T(8,128)(2,1)S(1)} %fusion.84), channel_id=1, source_target_pairs={{0,4},{4,0},{8,12},{12,8},{16,20},{20,16},{24,28},{28,24},{1,5},{5... | collective-permute-start | bytes 2359304 | tf_op jit(solution)/shard_map/ppermute | solution.py:109
  330.3 27.5 %collective-permute-start.31 = (bf16[256,1024]{1,0:T(8,128)(2,1)}, bf16[256,1024]{1,0:T(8,128)(2,1)}, u32[]{:S(2)}, u32[]{:S(2)}) collective-permute-start(bf16[256,1024]{1,0:T(8,128)(2,1)} %get-tuple-element.388), channel_id=1, source_target_pairs={{0,1},{1,0},{2,3},{3,2},{4,5},{5,4},{6,7},{7,6},{8,9},{9,8},{10,11... | collective-permute-start | bytes 1572872 | tf_op jit(solution)/shard_map/ppermute | solution.py:30
  332.9 24.9 %collective-permute-start.33 = (bf16[256,1024]{1,0:T(8,128)(2,1)}, bf16[256,1024]{1,0:T(8,128)(2,1)}, u32[]{:S(2)}, u32[]{:S(2)}) collective-permute-start(bf16[256,1024]{1,0:T(8,128)(2,1)} %fusion.66), channel_id=1, source_target_pairs={{0,2},{1,3},{2,0},{3,1},{4,6},{5,7},{6,4},{7,5},{8,10},{9,11},{10,... | collective-permute-start | bytes 1572872 | tf_op jit(solution)/shard_map/ppermute | solution.py:30
  335.0 24.8 %collective-permute-start.21 = (bf16[256,1024]{1,0:T(8,128)(2,1)}, bf16[256,1024]{1,0:T(8,128)(2,1)S(1)}, u32[]{:S(2)}, u32[]{:S(2)}) collective-permute-start(bf16[256,1024]{1,0:T(8,128)(2,1)} %fusion.70), channel_id=1, source_target_pairs={{0,2},{1,3},{2,0},{3,1},{4,6},{5,7},{6,4},{7,5},{8,10},{9,11},{10,... | collective-permute-start | bytes 1572872 | tf_op jit(solution)/shard_map/ppermute | solution.py:30
  353.4 24.5 %all-to-all-start.7 = ((bf16[4,128,768]{2,1,0:T(8,128)(2,1)}), bf16[4,128,768]{2,1,0:T(8,128)(2,1)}, u32[]{:S(2)}, u32[]{:S(2)}) async-start(bf16[4,128,768]{2,1,0:T(8,128)(2,1)} %fusion.56), calls=%async_computation.7 | async-start | bytes 1572864 | tf_op jit(solution)/shard_map/all_to_all | solution.py:111
  365.4 18.2 %collective-permute-start.38 = (bf16[256,1024]{1,0:T(8,128)(2,1)S(1)}, bf16[256,1024]{1,0:T(8,128)(2,1)S(1)}, u32[]{:S(2)}, u32[]{:S(2)}) collective-permute-start(bf16[256,1024]{1,0:T(8,128)(2,1)S(1)} %get-tuple-element.449), channel_id=1, source_target_pairs={{0,2},{1,3},{2,0},{3,1},{4,6},{5,7},{6,4},{7,5},{8,10},{9,11},{10,... | collective-permute-start | bytes 1572872 | tf_op jit(solution)/shard_map/ppermute | solution.py:30
  366.9 51.7 %collective-permute-start.37 = (bf16[256,1024]{1,0:T(8,128)(2,1)S(1)}, bf16[256,1024]{1,0:T(8,128)(2,1)}, u32[]{:S(2)}, u32[]{:S(2)}) collective-permute-start(bf16[256,1024]{1,0:T(8,128)(2,1)S(1)} %get-tuple-element.449), channel_id=1, source_target_pairs={{0,1},{1,0},{2,3},{3,2},{4,5},{5,4},{6,7},{7,6},{8,9},{9,8},{10,11... | collective-permute-start | bytes 1572872 | tf_op jit(solution)/shard_map/ppermute | solution.py:30
  383.6 35.0 %collective-permute-start.39 = (bf16[256,1024]{1,0:T(8,128)(2,1)S(1)}, bf16[256,1024]{1,0:T(8,128)(2,1)}, u32[]{:S(2)}, u32[]{:S(2)}) collective-permute-start(bf16[256,1024]{1,0:T(8,128)(2,1)S(1)} %collective-permute-done.38), channel_id=1, source_target_pairs={{0,1},{1,0},{2,3},{3,2},{4,5},{5,4},{6,7},{7,6},{8,9},{9,8},{10,11... | collective-permute-start | bytes 1572872 | tf_op jit(solution)/shard_map/ppermute | solution.py:30
  394.2 24.3 %collective-permute-start.34 = (bf16[256,512]{1,0:T(8,128)(2,1)S(1)}, bf16[256,512]{1,0:T(8,128)(2,1)S(1)}, u32[]{:S(2)}, u32[]{:S(2)}) collective-permute-start(bf16[256,512]{1,0:T(8,128)(2,1)S(1)} %get-tuple-element.399), channel_id=1, source_target_pairs={{0,1},{1,0},{2,3},{3,2},{4,5},{5,4},{6,7},{7,6},{8,9},{9,8},{10,11... | collective-permute-start | bytes 786440 | tf_op jit(solution)/shard_map/ppermute | solution.py:30
  394.8 23.8 %collective-permute-start.35 = (bf16[256,512]{1,0:T(8,128)(2,1)S(1)}, bf16[256,512]{1,0:T(8,128)(2,1)S(1)}, u32[]{:S(2)}, u32[]{:S(2)}) collective-permute-start(bf16[256,512]{1,0:T(8,128)(2,1)S(1)} %get-tuple-element.398), channel_id=1, source_target_pairs={{0,2},{1,3},{2,0},{3,1},{4,6},{5,7},{6,4},{7,5},{8,10},{9,11},{10,... | collective-permute-start | bytes 786440 | tf_op jit(solution)/shard_map/ppermute | solution.py:30
  396.5 22.1 %collective-permute-start.36 = (bf16[256,512]{1,0:T(8,128)(2,1)S(1)}, bf16[256,512]{1,0:T(8,128)(2,1)}, u32[]{:S(2)}, u32[]{:S(2)}) collective-permute-start(bf16[256,512]{1,0:T(8,128)(2,1)S(1)} %get-tuple-element.397), channel_id=1, source_target_pairs={{0,3},{1,2},{2,1},{3,0},{4,7},{5,6},{6,5},{7,4},{8,11},{9,10},{10,... | collective-permute-start | bytes 786440 | tf_op jit(solution)/shard_map/ppermute | solution.py:30
  412.3 26.7 %all-to-all-start.6 = ((f32[8,153,128]{2,1,0:T(8,128)}), f32[8,153,128]{2,1,0:T(8,128)}, u32[]{:S(2)}, u32[]{:S(2)}) async-start(f32[8,153,128]{2,1,0:T(8,128)} %pad_maximum_fusion.10), calls=%async_computation.6 | async-start | bytes 1310720 | tf_op jit(solution)/shard_map/all_to_all | solution.py:547
  421.3 16.2 %collective-permute-start.40 = (bf16[4,64,1024]{2,1,0:T(8,128)(2,1)S(1)}, bf16[4,64,1024]{2,1,0:T(8,128)(2,1)S(1)}, u32[]{:S(2)}, u32[]{:S(2)}) collective-permute-start(bf16[4,64,1024]{2,1,0:T(8,128)(2,1)S(1)} %fusion.89), channel_id=1, source_target_pairs={{0,4},{4,0},{8,12},{12,8},{16,20},{20,16},{24,28},{28,24},{1,5},{5... | collective-permute-start | bytes 1572872 | tf_op jit(solution)/shard_map/ppermute | solution.py:109
  421.5 22.6 %collective-permute-start.46 = (f32[32,1024]{1,0:T(8,128)S(1)}, f32[32,1024]{1,0:T(8,128)}, u32[]{:S(2)}, u32[]{:S(2)}) collective-permute-start(f32[32,1024]{1,0:T(8,128)S(1)} %convert_reduce_fusion.5), channel_id=1, source_target_pairs={{0,0},{1,8},{2,16},{3,24},{4,1},{5,9},{6,17},{7,25},{8,2},{9,10},{... | collective-permute-start | bytes 393224 | tf_op jit(solution)/shard_map/ppermute | solution.py:121
  439.0 19.0 %all-to-all-start.5 = ((bf16[4,64,1024]{2,1,0:T(8,128)(2,1)}), bf16[4,64,1024]{2,1,0:T(8,128)(2,1)S(1)}, u32[]{:S(2)}, u32[]{:S(2)}) async-start(bf16[4,64,1024]{2,1,0:T(8,128)(2,1)} %fusion.80), calls=%async_computation.5 | async-start | bytes 1048576 | tf_op jit(solution)/shard_map/all_to_all | solution.py:111
  458.1 16.0 %collective-permute-start.41 = (f32[64,1024]{1,0:T(8,128)S(1)}, f32[64,1024]{1,0:T(8,128)S(1)}, u32[]{:S(2)}, u32[]{:S(2)}) collective-permute-start(f32[64,1024]{1,0:T(8,128)S(1)} %convert_reduce_fusion.4), channel_id=1, source_target_pairs={{0,0},{1,8},{2,16},{3,24},{4,1},{5,9},{6,17},{7,25},{8,2},{9,10},{... | collective-permute-start | bytes 786440 | tf_op jit(solution)/shard_map/ppermute | solution.py:121
  (156 other events, 1800.6 us)
Sparse Core Ops, SparseCore 0:
  71.4 42.9 all-gather.3
  116.5 72.1 all-gather.5
  215.4 66.2 reduce-scatter.2
  285.1 70.6 reduce-scatter.4

commit v2 on v1

v2 whole, which is shorter than its diff:
```python
import math

import jax
import jax.numpy as jnp
from jax import lax
from jax.experimental import pallas as pl
from jax.experimental.pallas import tpu as pltpu
from jax.sharding import PartitionSpec as P

HD = 64
LANES = 128
BIAS_ROWS = 16
BF = jnp.bfloat16
F32 = jnp.float32
highest_precision = lax.Precision.HIGHEST
mask_value = -1e30


def product(left, right, left_dim, right_dim):
    return lax.dot_general(
        left, right, (((left_dim,), (right_dim,)), ((), ())), preferred_element_type=F32
    )


def dot32(left, right):
    return jnp.dot(left, right, preferred_element_type=F32)


def dot_nt(left, right):
    return lax.dot_general(left, right, (((1,), (1,)), ((), ())), preferred_element_type=F32)


def dot_tn(left, right):
    return lax.dot_general(left, right, (((0,), (0,)), ((), ())), preferred_element_type=F32)


fence = lax.optimization_barrier


def after(value, *others):
    return fence((value, others))[0]


def block_order(count):
    order, step = [0], count // 2
    while step >= 1:
        order = order + [d ^ step for d in order]
        step //= 2
    return order


def xor_sp(values, distance):
    size = lax.axis_size("sp")
    return lax.ppermute(values, "sp", [(i, i ^ distance) for i in range(size)])


def swap_utt(values):
    return lax.ppermute(values, "utt", [(i, i ^ 1) for i in range(lax.axis_size("utt"))])


def gather_sp(own):
    blocks, step = [own], lax.axis_size("sp") // 2
    while step >= 1:
        blocks = blocks + [xor_sp(b, step) for b in blocks]
        step //= 2
    return blocks


def exchange_sp(parts):
    order = block_order(len(parts))
    return [parts[0]] + [xor_sp(parts[i], order[i]) for i in range(1, len(parts))]


def in_device_order(blocks):
    order = block_order(len(blocks))
    stacked = jnp.stack([blocks[order.index(d)] for d in range(len(blocks))])
    me = lax.axis_index("sp")
    return [
        lax.dynamic_index_in_dim(stacked, me ^ a, 0, keepdims=False) for a in range(len(blocks))
    ]


def sum_sp(values):
    step = lax.axis_size("sp") // 2
    while step >= 1:
        values = values + xor_sp(values, step)
        step //= 2
    return values


def turn_utt(values, k):
    size = lax.axis_size("utt")
    high = size // 2
    routes = [(z * 2 + y, (z + k) % high * 2 + y) for z in range(high) for y in range(2)]
    return lax.ppermute(values, "utt", routes)


def line_blocks(own):
    return [own] + [turn_utt(own, k) for k in range(1, lax.axis_size("utt") // 2)]


def gather_line(own):
    return jnp.concatenate(line_blocks(own), axis=0)


def split_pair(parts, axis):
    low = lax.axis_index("utt") % 2
    keep = lax.dynamic_index_in_dim(parts, low, axis, keepdims=False)
    return keep, lax.dynamic_index_in_dim(parts, 1 - low, axis, keepdims=False)


def scatter_fast(parts):
    keep, send = split_pair(parts.reshape((-1, 2) + parts.shape[1:]), 1)
    return (keep.astype(F32) + swap_utt(send.astype(BF)).astype(F32)).astype(BF)


def scatter_slow(half):
    high = lax.axis_size("utt") // 2
    z = lax.axis_index("utt") // 2
    terms = [lax.dynamic_index_in_dim(half, z, 0, keepdims=False)]
    for k in range(1, high):
        piece = lax.dynamic_index_in_dim(half, (z + k) % high, 0, keepdims=False)
        terms.append(turn_utt(piece, k))
    return terms


def add_terms(terms):
    total = terms[0].astype(F32)
    for term in terms[1:]:
        total = total + term.astype(F32)
    return total


def entry(values, index):
    return lax.dynamic_index_in_dim(values, index, 0, keepdims=False)


def far_entries(values):
    me, far = lax.axis_index("sp"), lax.axis_size("sp") // 2
    return jnp.stack([entry(values, me ^ far), entry(values, me ^ far ^ 1)])


def exchange_far(values):
    return xor_sp(far_entries(values), lax.axis_size("sp") // 2)


def exchange_near(values, arrived):
    me = lax.axis_index("sp")
    last = xor_sp(jnp.stack([entry(values, me ^ 1), arrived[1]]), 1)
    return [entry(values, me), arrived[0], last[0], last[1]]


def split_exchange_sp(values):
    return jnp.stack(in_device_order(exchange_near(values, exchange_far(values))))


class Pieces:
    def __init__(self):
        self.arrays, self.starts, self.sizes = [], [], []

    def add(self, array, first_rows, size):
        self.arrays.append(array)
        self.starts.append(first_rows)
        self.sizes.append(size)

    def offsets(self):
        return jnp.stack([start for starts in self.starts for start in starts]).astype(jnp.int32)

    def count(self):
        return sum(len(starts) for starts in self.starts)

    def copies(self, offset_ref, refs, whole_ref, sems):
        made, n = [], 0
        for ref, starts, size in zip(refs, self.starts, self.sizes):
            for i in range(len(starts)):
                first = pl.multiple_of(offset_ref[n], size)
                made.append(
                    pltpu.make_async_copy(
                        ref.at[pl.ds(i * size, size)], whole_ref.at[pl.ds(first, size)], sems.at[n]
                    )
                )
                n += 1
        return made


def line_indices(flip):
    size = lax.axis_size("utt")
    high = size // 2
    u = lax.axis_index("utt")
    z, y = u // 2, u % 2
    return [(z - k + high) % high * 2 + (1 - y if flip else y) for k in range(high)]


def whole_pieces(arrays, rows):
    n_s, me = lax.axis_size("sp"), lax.axis_index("sp")
    pieces = Pieces()
    for array, d, owners, shift, size in arrays:
        pieces.add(array, [(i * n_s + (me ^ d)) * rows + shift for i in owners], size)
    return pieces


def to_owner(values):
    n_u, n_s = lax.axis_size("utt"), lax.axis_size("sp")
    routes = []
    for p in range(n_u):
        for s in range(n_s):
            routes.append((p * n_s + s, s * n_u + p))
    return lax.ppermute(values, ("utt", "sp"), routes)


def owned(values):
    n = lax.axis_size("utt") * lax.axis_size("sp")
    j = lax.axis_index("utt") * lax.axis_size("sp") + lax.axis_index("sp")
    size = values.shape[-1] // n
    return lax.dynamic_slice_in_dim(values, j * size, size, values.ndim - 1)


def norm_parts(values):
    mean_row = jnp.mean(values, axis=-1, keepdims=True)
    centered = values - mean_row
    variance = jnp.mean(centered * centered, axis=-1, keepdims=True)
    scale = lax.rsqrt(variance + 1e-06)
    return centered * scale, scale


def norm_back(normal, scale, grads):
    mean_grad = jnp.mean(grads, axis=-1, keepdims=True)
    mean_both = jnp.mean(grads * normal, axis=-1, keepdims=True)
    return (grads - mean_grad - normal * mean_both) * scale


def rotary_tables(position):
    half_head = HD // 2
    inverse = jnp.exp(jnp.arange(half_head, dtype=F32) * (-2.0 * math.log(10000.0) / HD))
    angle_arg = position.astype(F32)[:, None] * inverse[None, :]
    cosine, sine = jnp.cos(angle_arg), jnp.sin(angle_arg)
    return (
        jnp.concatenate([cosine] * 4, axis=1),
        jnp.concatenate([-sine, sine, -sine, sine], axis=1),
    )


def utterance_layout(lengths_row, frame_ids):
    ends_at = jnp.cumsum(lengths_row)
    starts_at = ends_at - lengths_row
    inside = (frame_ids[:, None] >= starts_at[None, :]) & (frame_ids[:, None] < ends_at[None, :])
    segment = jnp.sum(jnp.where(frame_ids[:, None] >= ends_at[None, :], 1, 0), axis=1).astype(
        jnp.int32
    )
    position = frame_ids - jnp.sum(jnp.where(inside, starts_at[None, :], 0), axis=1)
    return inside, segment, position


QUERY_ROWS = 512


def any_refs(count):
    return [pl.BlockSpec(memory_space=pltpu.HBM)] * count


def smem_ref():
    return pl.BlockSpec(memory_space=pltpu.SMEM)


def vmem_ref():
    return pl.BlockSpec(memory_space=pltpu.VMEM)


def placed_product(lefts, pieces, depth):
    n, count = len(pieces.arrays), pieces.count()
    rows = lefts[0].shape[0]
    width = pieces.arrays[0].shape[1]

    def kernel(offset_ref, *refs):
        piece_refs, left_refs = refs[:n], refs[n : n + len(lefts)]
        whole_ref, base_ref, sems = refs[n + len(lefts) :]
        copies = pieces.copies(offset_ref, piece_refs, whole_ref, sems)
        for copy in copies:
            copy.start()
        for copy in copies:
            copy.wait()
        total, first = None, 0
        for left_ref in left_refs:
            last = first + left_ref.shape[1]
            term = product(left_ref[...], whole_ref[first:last, :], 1, 0)
            total = term if total is None else total + term
            first = last
        base_ref[...] = total

    return pl.pallas_call(
        kernel,
        out_shape=(
            jax.ShapeDtypeStruct((depth, width), BF),
            jax.ShapeDtypeStruct((rows, width), F32),
        ),
        in_specs=[smem_ref()] + any_refs(n) + [vmem_ref()] * len(lefts),
        out_specs=(vmem_ref(),) * 2,
        scratch_shapes=[pltpu.SemaphoreType.DMA((count,))],

        cost_estimate=pl.CostEstimate(
            flops=2 * rows * depth * width,
            bytes_accessed=4 * depth * width + 2 * rows * (depth + 2 * width),
            transcendentals=0,
        ),
        name="placed_product",
    )(pieces.offsets(), *pieces.arrays, *lefts)


def turn_halves(values, cosine, sine):
    half, cols = HD // 2, values.shape[1]
    first = lax.broadcasted_iota(jnp.int32, values.shape, 1) % HD < half
    swapped = jnp.where(
        first, pltpu.roll(values, cols - half, 1), pltpu.roll(values, half, 1)
    )
    repeats = cols // cosine.shape[1]
    wide = lambda t: jnp.concatenate([t] * repeats, axis=1) if repeats > 1 else t
    return values * wide(cosine) + swapped * wide(sine)


def attend(normed_blocks, weight, bias, cosine, sine, segment):
    blocks, width = len(normed_blocks), normed_blocks[0].shape[1]
    rows = normed_blocks[0].shape[0]
    total = blocks * rows
    cols = weight.shape[1] // 3
    heads = cols // HD
    block = min(QUERY_ROWS, total)

    def kernel(*refs):
        block_refs = refs[:blocks]
        (
            weight_ref,
            cos_from,
            sin_from,
            b_ref,
            segc_ref,
            segr_ref,
            x_ref,
            q_ref,
            k_ref,
            v_ref,
            o_ref,
            lse_ref,
            vt_ref,
            bias_ref,
            w_ref,
            cos_ref,
            sin_ref,
            sems,
        ) = refs[blocks:]
        sources = [weight_ref, cos_from, sin_from, *block_refs]
        targets = [w_ref, cos_ref, sin_ref] + [
            x_ref.at[pl.ds(i * rows, rows)] for i in range(blocks)
        ]
        copies = [
            pltpu.make_async_copy(sources[i], targets[i], sems.at[i]) for i in range(3 + blocks)
        ]
        for copy in copies:
            copy.start()

        for copy in copies:
            copy.wait()

        def project(i, carried):
            at = pl.ds(pl.multiple_of(i * block, block), block)
            three = product(x_ref[at, :], w_ref[...], 1, 0) + b_ref[...]
            cosine, sine = cos_ref[at, :], sin_ref[at, :]
            q_ref[at, :] = turn_halves(three[:, :cols], cosine, sine).astype(BF)
            k_ref[at, :] = turn_halves(three[:, cols : 2 * cols], cosine, sine).astype(BF)
            v_ref[at, :] = three[:, 2 * cols :].astype(BF)
            return carried

        lax.fori_loop(0, total // block, project, 0)
        vt_ref[...] = v_ref[...].T

        def one(i, carried):
            row = pl.multiple_of(i * block, block)
            same = segc_ref[...] == segr_ref[:, pl.ds(row, block)]
            bias_ref[...] = jnp.where(same, 0.0, mask_value)
            outs = []
            for h in range(heads):
                c = slice(h * HD, (h + 1) * HD)
                scores = product(k_ref[:, c], q_ref[pl.ds(row, block), c], 1, 1)
                scores = scores * (HD**-0.5) + bias_ref[...]
                top = jnp.max(scores, axis=0, keepdims=True)
                exps = jnp.exp(scores - top)
                totals = jnp.sum(exps, axis=0, keepdims=True)
                outs.append(product(vt_ref[c, :], exps.astype(BF), 1, 0) * (1.0 / totals))
                lse_ref[h : h + 1, pl.ds(row, block)] = top + jnp.log(totals)
            o_ref[pl.ds(row, block), :] = jnp.concatenate(outs, axis=0).T.astype(BF)
            return carried

        lax.fori_loop(0, total // block, one, 0)

    return pl.pallas_call(
        kernel,
        out_shape=(
            jax.ShapeDtypeStruct((total, width), BF),
            jax.ShapeDtypeStruct((total, cols), BF),
            jax.ShapeDtypeStruct((total, cols), BF),
            jax.ShapeDtypeStruct((total, cols), BF),
            jax.ShapeDtypeStruct((total, cols), BF),
            jax.ShapeDtypeStruct((heads, total), F32),
        ),
        in_specs=any_refs(blocks + 3) + [vmem_ref()] * 3,
        out_specs=(vmem_ref(),) * 6,
        scratch_shapes=[
            pltpu.VMEM((cols, total), BF),
            pltpu.VMEM((total, block), F32),
            pltpu.VMEM(weight.shape, BF),
            pltpu.VMEM(cosine.shape, F32),
            pltpu.VMEM(cosine.shape, F32),
            pltpu.SemaphoreType.DMA((blocks + 3,)),
        ],

        cost_estimate=pl.CostEstimate(
            flops=4 * total * total * cols + 6 * total * width * cols,
            bytes_accessed=8 * total * cols + 2 * total * width + 6 * width * cols,
            transcendentals=heads * total * total,
        ),
        name="attend_forward",
    )(
        *normed_blocks,
        weight,
        cosine,
        sine,
        bias[None, :],
        segment[:, None],
        segment[None, :],
    )


def attend_back(queries, keys, values, grad_blocks, log_totals, cosine, sine, segment):
    total, cols = queries.shape
    heads = cols // HD
    block = min(QUERY_ROWS, total)
    blocks, rows = len(grad_blocks), grad_blocks[0].shape[0]

    def kernel(*refs):
        big_refs, block_refs = refs[:5], refs[5 : 5 + blocks]
        (
            lse_ref,
            segc_ref,
            segr_ref,
            d_ref,
            q_ref,
            k_ref,
            v_ref,
            cos_ref,
            sin_ref,
            g_ref,
            kt_ref,
            bias_ref,
            dk_sum,
            dv_sum,
            sems,
        ) = refs[5 + blocks :]
        held = (q_ref, k_ref, v_ref, cos_ref, sin_ref)
        copies = [pltpu.make_async_copy(big_refs[i], held[i], sems.at[i]) for i in range(5)] + [
            pltpu.make_async_copy(block_refs[i], g_ref.at[pl.ds(i * rows, rows)], sems.at[5 + i])
            for i in range(blocks)
        ]
        for copy in copies:
            copy.start()
        dk_sum[...] = jnp.zeros_like(dk_sum)
        dv_sum[...] = jnp.zeros_like(dv_sum)
        for copy in copies:
            copy.wait()
        kt_ref[...] = k_ref[...].T

        def one(i, carried):
            row = pl.multiple_of(i * block, block)
            at = pl.ds(row, block)
            same = segc_ref[...] == segr_ref[:, at]
            bias_ref[...] = jnp.where(same, 0.0, mask_value)
            outs = []
            for h in range(heads):
                c = slice(h * HD, (h + 1) * HD)
                query, grad = q_ref[at, c], g_ref[at, c]
                scores = product(k_ref[:, c], query, 1, 1) * (HD**-0.5) + bias_ref[...]
                probs = jnp.exp(scores - lse_ref[h : h + 1, at])
                both = probs * product(v_ref[:, c], grad, 1, 1)
                inner = jnp.sum(both, axis=0, keepdims=True)
                grad_scores = (both - probs * inner).astype(BF)
                dv_sum[:, c] += product(probs.astype(BF), grad, 1, 0)
                dk_sum[:, c] += product(grad_scores, query, 1, 0)
                outs.append(product(kt_ref[c, :], grad_scores, 1, 0))
            grad_query = (jnp.concatenate(outs, axis=0) * (HD**-0.5)).T.astype(BF).astype(F32)
            d_ref[at, :cols] = turn_halves(grad_query, cos_ref[at, :], -sin_ref[at, :]).astype(BF)
            return carried

        lax.fori_loop(0, total // block, one, 0)
        grad_key = (dk_sum[...] * (HD**-0.5)).astype(BF).astype(F32)
        d_ref[:, cols : 2 * cols] = turn_halves(grad_key, cos_ref[...], -sin_ref[...]).astype(BF)
        d_ref[:, 2 * cols :] = dv_sum[...].astype(BF)

    return pl.pallas_call(
        kernel,
        out_shape=jax.ShapeDtypeStruct((total, 3 * cols), BF),
        in_specs=any_refs(5 + blocks) + [vmem_ref()] * 3,
        out_specs=vmem_ref(),
        scratch_shapes=[pltpu.VMEM((total, cols), BF)] * 3
        + [pltpu.VMEM(cosine.shape, F32)] * 2
        + [
            pltpu.VMEM((total, cols), BF),
            pltpu.VMEM((cols, total), BF),
            pltpu.VMEM((total, block), F32),
            pltpu.VMEM((total, cols), F32),
            pltpu.VMEM((total, cols), F32),
            pltpu.SemaphoreType.DMA((5 + blocks,)),
        ],

        cost_estimate=pl.CostEstimate(
            flops=10 * total * total * cols,
            bytes_accessed=14 * total * cols,
            transcendentals=heads * total * total,
        ),
        name="attend_backward",
    )(
        queries,
        keys,
        values,
        cosine,
        sine,
        *grad_blocks,
        log_totals,
        segment[:, None],
        segment[None, :],
    )


def gelu_both(values):
    root = math.sqrt(2.0 / math.pi)
    square = values * values
    tanh = jnp.tanh(root * (values + 0.044715 * (values * square)))
    half = 0.5 * (1.0 + tanh)
    slope = root * (1.0 + 3 * 0.044715 * square)
    return values * half, half + 0.5 * values * (1.0 - tanh * tanh) * slope


def feed_forward(normed_blocks, grad_blocks, weights, up_bias, up_rows):
    sources = list(normed_blocks) + list(grad_blocks)
    count, width = len(sources), normed_blocks[0].shape[1]
    total = sum(block.shape[0] for block in normed_blocks)
    parts, both_rows, ff = weights.shape
    down_rows = both_rows - up_rows
    group = max(1, 256 // down_rows)
    block, half = group * down_rows, total // 2
    steps = ff // block

    def kernel(*refs):
        (
            weight_from,
            b_ref,
            act_ref,
            gh_ref,
            sum_ref,
            keep_ref,
            send_ref,
            x_ref,
            g_ref,
            acc_ref,
            w_ref,
            hidden_ref,
            active_ref,
            sems,
        ) = refs[count:]
        step = pl.program_id(0)
        copies, first = [], 0
        for i, ref in enumerate(refs[:count]):
            whole = x_ref if i < len(normed_blocks) else g_ref
            at = pl.ds(first % total, ref.shape[0])
            copies.append(pltpu.make_async_copy(ref, whole.at[at], sems.at[i]))
            first += ref.shape[0]
        copies.append(pltpu.make_async_copy(weight_from, w_ref, sems.at[count]))

        @pl.when(step == 0)
        def _():
            for copy in copies:
                copy.start()
            for copy in copies:
                copy.wait()

        def up_of(i):
            at = pl.ds(pl.multiple_of(i * block, block), block)
            return w_ref[:, :up_rows, at].reshape(width, block)

        now, before = jnp.minimum(step, steps - 1), jnp.maximum(step - 1, 0)
        slot, other = step % 2, (step + 1) % 2
        hidden_ref[slot] = product(x_ref[...], up_of(now), 1, 0) + b_ref[now]
        down = w_ref[pl.ds(now * group, group), up_rows:, :].reshape(block, width)
        active_ref[slot] = product(g_ref[...], down, 1, 1)

        active, slope = gelu_both(hidden_ref[other])
        act_ref[...] = active.astype(BF)
        grad_hidden = (active_ref[other] * slope).astype(BF)
        gh_ref[...] = grad_hidden
        sum_ref[...] = jnp.sum(grad_hidden.astype(F32), axis=0, keepdims=True)
        part = product(grad_hidden, up_of(before), 1, 1)

        @pl.when(step <= 1)
        def _():
            acc_ref[...] = part

        @pl.when(step > 1)
        def _():
            acc_ref[...] += part

        @pl.when(step == steps)
        def _():
            keep_ref[...] = acc_ref[:half, :]
            send_ref[...] = acc_ref[half:, :].astype(BF)

    fixed = lambda i: (0, 0)
    behind = lambda i: (0, jnp.maximum(i - 1, 0))
    return pl.pallas_call(
        kernel,
        grid=(steps + 1,),
        out_shape=(
            jax.ShapeDtypeStruct((total, ff), BF),
            jax.ShapeDtypeStruct((total, ff), BF),
            jax.ShapeDtypeStruct((1, ff), F32),
            jax.ShapeDtypeStruct((half, width), F32),
            jax.ShapeDtypeStruct((half, width), BF),
        ),
        in_specs=any_refs(count + 1) + [pl.BlockSpec((steps, 1, block), lambda i: (0, 0, 0))],
        out_specs=(
            pl.BlockSpec((total, block), behind),
            pl.BlockSpec((total, block), behind),
            pl.BlockSpec((1, block), behind),
            pl.BlockSpec((half, width), fixed),
            pl.BlockSpec((half, width), fixed),
        ),
        scratch_shapes=[
            pltpu.VMEM((total, width), BF),
            pltpu.VMEM((total, width), BF),
            pltpu.VMEM((total, width), F32),
            pltpu.VMEM(weights.shape, BF),
            pltpu.VMEM((2, total, block), F32),
            pltpu.VMEM((2, total, block), F32),
            pltpu.SemaphoreType.DMA((count + 1,)),
        ],

        cost_estimate=pl.CostEstimate(
            flops=6 * total * width * ff,
            bytes_accessed=2 * (4 * total * width + 2 * total * ff + 2 * width * ff),
            transcendentals=total * ff,
        ),
        name="feed_forward",
    )(*sources, weights, up_bias.reshape(steps, 1, block))


def feed_forward_weights(normed_blocks, grad_hidden, active, grad_blocks, weights, up_rows):
    sources = list(normed_blocks) + list(grad_blocks)
    count, width = len(sources), normed_blocks[0].shape[1]
    total, ff = active.shape
    parts = weights.shape[0]
    down_rows = ff // parts
    group = max(1, min(parts, 256 // up_rows))
    steps = parts // group
    tall, near = total // steps, steps // 2

    def kernel(*refs):
        (
            gh_from,
            weight_from,
            a_ref,
            r_ref,
            o_ref,
            keep_ref,
            send_ref,
            x_ref,
            g_ref,
            gh_ref,
            down_ref,
            sems,
        ) = refs[count:]
        step = pl.program_id(0)
        copies, first = [], 0
        for i, ref in enumerate(refs[:count]):
            whole = x_ref if i < len(normed_blocks) else g_ref
            at = pl.ds(first % total, ref.shape[0])
            copies.append(pltpu.make_async_copy(ref, whole.at[at], sems.at[i]))
            first += ref.shape[0]
        copies.append(pltpu.make_async_copy(gh_from, gh_ref, sems.at[count]))
        copies.append(
            pltpu.make_async_copy(weight_from.at[:, up_rows:, :], down_ref, sems.at[count + 1])
        )

        @pl.when(step == 0)
        def _():
            for copy in copies:
                copy.start()
            for copy in copies:
                copy.wait()

        at = pl.ds(pl.multiple_of(step * (group * up_rows), group * up_rows), group * up_rows)
        up = product(x_ref[:, at], gh_ref[...], 0, 0).astype(BF)
        down = product(a_ref[...], g_ref[...], 0, 0).astype(BF)
        for i in range(group):
            o_ref[i, :up_rows, :] = up[i * up_rows : (i + 1) * up_rows]
            o_ref[i, up_rows:, :] = down[i * down_rows : (i + 1) * down_rows]
        result = product(r_ref[...], down_ref[...].reshape(ff, width), 1, 0)

        @pl.when(step < near)
        def _():
            keep_ref[...] = result

        @pl.when(step >= near)
        def _():
            send_ref[...] = result.astype(BF)

    return pl.pallas_call(
        kernel,
        grid=(steps,),
        out_shape=(
            jax.ShapeDtypeStruct((parts, up_rows + down_rows, width), BF),
            jax.ShapeDtypeStruct((total // 2, width), F32),
            jax.ShapeDtypeStruct((total // 2, width), BF),
        ),
        in_specs=any_refs(count + 2)
        + [
            pl.BlockSpec((total, group * down_rows), lambda i: (0, i)),
            pl.BlockSpec((tall, ff), lambda i: (i, 0)),
        ],
        out_specs=(
            pl.BlockSpec((group, up_rows + down_rows, width), lambda i: (i, 0, 0)),
            pl.BlockSpec((tall, width), lambda i: (jnp.minimum(i, near - 1), 0)),
            pl.BlockSpec((tall, width), lambda i: (jnp.maximum(i - near, 0), 0)),
        ),
        scratch_shapes=[
            pltpu.VMEM((total, width), BF),
            pltpu.VMEM((total, width), BF),
            pltpu.VMEM((total, ff), BF),
            pltpu.VMEM((parts, down_rows, width), BF),
            pltpu.SemaphoreType.DMA((count + 2,)),
        ],
        cost_estimate=pl.CostEstimate(
            flops=6 * total * width * ff,
            bytes_accessed=2 * (2 * total * (width + ff) + 2 * width * ff),
            transcendentals=0,
        ),
        name="feed_forward_weights",
    )(*sources, grad_hidden, weights, active, active)


def own_time_features(times, first_col, col_count, model_width):
    half_width = model_width // 2
    cols = first_col + jnp.arange(col_count, dtype=jnp.int32)
    is_sine = cols < half_width
    steps_row = jnp.where(is_sine, cols, cols - half_width).astype(F32)
    frequency = jnp.exp(steps_row * (-math.log(10000.0) / (half_width - 1)))
    phase_arg = 1000.0 * times[:, None] * frequency[None, :]
    features = jnp.where(is_sine[None, :], jnp.sin(phase_arg), jnp.cos(phase_arg))
    return jax.nn.silu(features).astype(BF)


def pad_rows(vector):
    rows = -(-vector.shape[-1] // LANES)
    return jnp.pad(vector, (0, rows * LANES - vector.shape[-1])).reshape(rows, LANES)


def body(
    frames,
    skip_frames,
    lengths,
    flow_time,
    skip_weight,
    adaln_weight,
    adaln_bias,
    qkv_weight,
    qkv_bias,
    output_weight,
    output_bias,
    up_weight,
    up_bias,
    down_weight,
    down_bias,
    out_grad,
):
    n_u, n_s = lax.axis_size("utt"), lax.axis_size("sp")
    u, s = lax.axis_index("utt"), lax.axis_index("sp")
    n_all = n_u * n_s
    me = u * n_s + s
    rows, width = frames.shape
    per_group = lengths.shape[1]
    ff = up_weight.shape[1]
    part_width = width // n_s
    part_ff = ff // n_s
    lengths_row = lengths[0]

    all_ids = jnp.concatenate(
        [(s ^ d) * rows + jnp.arange(rows, dtype=jnp.int32) for d in block_order(n_s)]
    )
    inside_all, segment_all, position_all = utterance_layout(lengths_row, all_ids)
    inside = inside_all[:rows]

    cols = qkv_weight.shape[0]
    slot, out_slot = skip_weight.shape[0], output_weight.shape[0]
    far = n_s // 2
    bias_sizes = [qkv_bias.shape[0], output_bias.shape[0], up_bias.shape[0], down_bias.shape[0]]
    bias_own = pad_rows(
        jnp.concatenate([qkv_bias, output_bias, up_bias, down_bias]).astype(F32)
    )
    qkv_split = qkv_weight.reshape(cols, 3, n_s, part_width).transpose(2, 0, 1, 3)
    up_split = up_weight.reshape(cols, n_u, n_s, ff // n_all).transpose(2, 0, 1, 3)
    both_split = jnp.concatenate(
        [qkv_split.reshape(n_s, cols, 3 * part_width), up_split.reshape(n_s, cols, part_ff)], axis=2
    )
    skip_blocks = line_blocks(skip_weight)
    flow_row = jnp.pad(flow_time, ((0, 0), (0, LANES - per_group)))
    first_rows = jnp.concatenate([flow_row, bias_own], axis=0)
    first_rows = lax.all_to_all(
        jnp.broadcast_to(first_rows[None], (n_u,) + first_rows.shape), "utt", 0, 0, tiled=True
    )
    both_mine = lax.all_to_all(after(both_split, first_rows), "sp", 0, 0, tiled=True)
    part = n_u * slot
    chosen = jnp.arange(2 * width, dtype=jnp.int32)
    chosen = chosen % part // slot * (slot * n_s) + chosen // part * slot + chosen % slot
    selection = (jnp.arange(2 * width, dtype=jnp.int32)[:, None] == chosen[None, :]).astype(BF)
    joined_split = dot32(jnp.concatenate([frames, skip_frames], axis=1), selection).astype(BF)
    joined_split = joined_split.reshape(rows, n_s, part).transpose(1, 0, 2)
    joined_sent = far_entries(joined_split)
    skip_blocks, both_mine, first_rows, joined_split, joined_sent = fence(
        (skip_blocks, both_mine, first_rows, joined_split, joined_sent)
    )
    skip_line = jnp.concatenate(skip_blocks, axis=0)
    both_mine = both_mine.reshape(n_s * cols, -1)
    my_qkv = lax.all_gather(both_mine[:, : 3 * part_width], "utt", axis=0, tiled=True)
    ff_lines = lax.all_gather(
        jnp.concatenate([both_mine[:, 3 * part_width :], down_weight], axis=0), "utt", axis=0
    )

    times = first_rows[:, 0, :per_group].reshape(n_u * per_group)
    feature_rows = adaln_weight.shape[0]
    silu_own = own_time_features(times, me * feature_rows, feature_rows, width)
    table_width = adaln_weight.shape[1]
    mod_terms = dot32(silu_own, adaln_weight)
    bias_cols = lax.dynamic_update_slice(
        jnp.zeros((table_width,), F32), adaln_bias.astype(F32), (me * adaln_bias.shape[0],)
    )
    mod_terms = (mod_terms + bias_cols[None, :]).reshape(n_u, per_group, 6, width)
    mod_terms = mod_terms.transpose(0, 2, 1, 3).reshape(n_u, 6 * per_group, width)

    high, half = skip_line.shape[0] // slot, slot // 2
    rows_of = lambda x: x.reshape(high, slot, width)
    over_sp, over_utt = xor_sp(skip_line, far), swap_utt(skip_line)
    joined_far = xor_sp(joined_sent, far)
    near_line = xor_sp(skip_line, 1)
    mod_terms = lax.all_to_all(mod_terms, "utt", 0, 0, tiled=True)
    cosine, sine = rotary_tables(position_all)
    over_sp, over_utt, joined_far, near_line, mod_terms, cosine, sine = fence(
        (over_sp, over_utt, joined_far, near_line, mod_terms, cosine, sine)
    )
    top = xor_sp(rows_of(over_utt)[:, :half].reshape(high * half, width), far)
    bottom = swap_utt(rows_of(over_sp)[:, half:].reshape(high * half, width))
    near_sp, near_utt = xor_sp(over_sp, 1), xor_sp(over_utt, 1)
    table_rows = 6 * per_group
    bias_own = first_rows[:, 1:].reshape(-1, width)
    message = jnp.concatenate([jnp.sum(mod_terms, axis=0), bias_own], axis=0)
    message_far = xor_sp(message, far)
    output_blocks = lax.all_to_all(
        jnp.broadcast_to(after(output_weight, over_sp)[None], (n_u, out_slot, width)),
        "utt",
        0,
        0,
        tiled=True,
    ).reshape(n_u * out_slot, width)
    top, bottom, near_sp, near_utt, message_far, my_qkv = fence(
        (top, bottom, near_sp, near_utt, message_far, my_qkv)
    )
    corner = jnp.concatenate([top, bottom], axis=0)
    message = jnp.concatenate(
        [message[:table_rows] + message_far[:table_rows], bias_own, message_far[table_rows:]], axis=0
    )
    corner, message = fence((corner, message))
    near_corner, message_near = fence((xor_sp(corner, 1), xor_sp(message, 1)))
    mod_table = message[:table_rows] + message_near[:table_rows]
    bias_blocks = [
        m.reshape(2, n_u, -1)[i]
        for m in (message[table_rows:], message_near[table_rows:])
        for i in range(2)
    ]
    here, there = line_indices(False), line_indices(True)
    skip_pieces = Pieces()
    whole_row = lambda i, distance: (i * n_s + (s ^ distance)) * slot
    for array, owners, distance in (
        (skip_line, here, 0),
        (over_sp, here, far),
        (over_utt, there, 0),
        (near_line, here, 1),
        (near_sp, here, far ^ 1),
        (near_utt, there, 1),
    ):
        skip_pieces.add(array, [whole_row(i, distance) for i in owners], slot)
    for array, distance in ((corner, far), (near_corner, far ^ 1)):
        skip_pieces.add(
            array,
            [whole_row(i, distance) for i in there]
            + [whole_row(i, distance) + half for i in there],
            half,
        )

    def expand(block, segment):
        table = mod_table[block * per_group : (block + 1) * per_group]
        result = table[per_group - 1][None, :]
        for k in range(per_group - 2, -1, -1):
            result = jnp.where(segment[:, None] == k, table[k][None, :], result)
        return result

    def segment_sums(values):
        return jnp.stack(
            [jnp.sum(jnp.where(inside[:, k][:, None], values, 0.0), axis=0) for k in range(per_group)]
        )

    segment_own = segment_all[:rows]
    scale_attn, gate_attn, shift_ffn, scale_ffn, gate_ffn = [
        expand(i, segment_own) for i in range(1, 6)
    ]

    grad_out = out_grad.astype(F32)
    grad_result = (gate_ffn * grad_out).astype(BF)
    grad_result_far = xor_sp(grad_result, far)
    full_skip, base_rows = placed_product([frames, skip_frames], skip_pieces, 2 * width)
    base_rows, my_qkv, grad_result_far = fence((base_rows, my_qkv, grad_result_far))
    base_norm, base_scale = norm_parts(base_rows)
    normed = (base_norm * (1.0 + scale_attn) + expand(0, segment_own)).astype(BF)
    far_normed = xor_sp(normed, far)
    far_normed, output_blocks = fence((far_normed, output_blocks))
    two_normed = jnp.concatenate([normed, far_normed], axis=0)
    near_normed = xor_sp(two_normed, 1)
    joined_mine = exchange_near(joined_split, joined_far)
    near_normed, joined_mine = fence((near_normed, joined_mine))
    output_far = xor_sp(output_blocks, far)
    bias_all = jnp.stack(in_device_order(bias_blocks), axis=1).reshape(n_u, n_s, -1)
    offsets = [0]
    for size in bias_sizes:
        offsets.append(offsets[-1] + size)
    full_qkv_bias, full_output_bias, full_up_bias, full_down_bias = [
        bias_all[:, :, offsets[i] : offsets[i + 1]].reshape(-1) for i in range(4)
    ]
    my_qkv_bias = lax.dynamic_slice_in_dim(
        full_qkv_bias.reshape(3, width), s * part_width, part_width, 1
    ).reshape(-1)
    my_up_bias = lax.dynamic_index_in_dim(
        full_up_bias.reshape(n_u, n_s, -1), s, 1, keepdims=False
    ).reshape(-1)

    normed_all, query_rows, key_rows, value_rows, attended_heads, log_totals = attend(
        [two_normed, near_normed], my_qkv, my_qkv_bias, cosine, sine, segment_all
    )
    attended_heads, output_far = fence((attended_heads, output_far))
    arrived = exchange_sp([attended_heads[i * rows : (i + 1) * rows] for i in range(n_s)])
    output_near = xor_sp(jnp.concatenate([output_blocks, output_far], axis=0), 1)
    grad_result_near = xor_sp(jnp.concatenate([grad_result, grad_result_far], axis=0), 1)
    arrived, output_near, grad_result_near = fence((arrived, output_near, grad_result_near))
    output_pieces = whole_pieces(
        [
            (output_blocks, 0, range(n_u), 0, out_slot),
            (output_far, far, range(n_u), 0, out_slot),
        ],
        out_slot,
    )
    output_pieces.add(
        output_near,
        [(i * n_s + (s ^ 1)) * out_slot for i in range(n_u)]
        + [(i * n_s + (s ^ 1 ^ far)) * out_slot for i in range(n_u)],
        out_slot,
    )
    attended = jnp.concatenate(in_device_order(arrived), axis=1)
    full_output, branch = placed_product([attended], output_pieces, width)
    branch = branch + full_output_bias[None, :]
    middle = base_rows + gate_attn * branch
    middle_norm, middle_scale = norm_parts(middle)
    normed_ffn = (middle_norm * (1.0 + scale_ffn) + shift_ffn).astype(BF)

    half_rows = n_s * rows // 2
    far_ffn = xor_sp(normed_ffn, far)
    two_ffn = jnp.concatenate([normed_ffn, far_ffn], axis=0)
    near_ffn = xor_sp(two_ffn, 1)
    ffn_blocks = [two_ffn, near_ffn]
    grad_result_blocks = [grad_result, grad_result_far, grad_result_near]
    active, grad_hidden, grad_up_bias, kept, sent = feed_forward(
        ffn_blocks, grad_result_blocks, ff_lines, my_up_bias, n_s * cols
    )
    arrived = xor_sp(sent, 1)
    far_sent = (kept[rows:] + arrived[rows:].astype(F32)).astype(BF)
    far_sent, active, grad_hidden = fence((far_sent, active, grad_hidden))
    far_sum = xor_sp(far_sent, n_s // 2)

    ff_grads, result_kept, sent = feed_forward_weights(
        ffn_blocks, grad_hidden, active, grad_result_blocks, ff_lines, n_s * cols
    )
    far_sum, result_kept, sent, ff_grads = fence((far_sum, result_kept, sent, ff_grads))
    grad_normed_ffn = kept[:rows] + arrived[:rows].astype(F32) + far_sum.astype(F32)
    ff_mine = lax.psum_scatter(ff_grads, "utt", scatter_dimension=0, tiled=True)[0]
    grad_middle = grad_out + norm_back(
        middle_norm, middle_scale, grad_normed_ffn * (1.0 + scale_ffn)
    )
    grad_branch = (gate_attn * grad_middle).astype(BF)
    grad_attended = dot_nt(grad_branch, full_output).astype(BF)
    grad_heads = exchange_sp(
        [
            lax.dynamic_slice_in_dim(grad_attended, (s ^ d) * part_width, part_width, 1)
            for d in block_order(n_s)
        ]
    )
    result_arrived = xor_sp(after(sent, grad_attended), 1)
    grad_heads, result_arrived, grad_branch = fence((grad_heads, result_arrived, grad_branch))
    far_branch = xor_sp(grad_branch, far)
    result_sent = (result_kept[rows:] + result_arrived[rows:].astype(F32)).astype(BF)

    grad_projected = attend_back(
        query_rows, key_rows, value_rows, grad_heads, log_totals, cosine, sine, segment_all
    )
    grad_projected, far_branch = fence((grad_projected, far_branch))
    sent = product(grad_projected[half_rows:], my_qkv, 1, 1).astype(BF)
    kept = product(grad_projected[:half_rows], my_qkv, 1, 1)
    arrived = xor_sp(sent, 1)
    far_sent = (kept[rows:] + arrived[rows:].astype(F32)).astype(BF)
    far_sent, projected_late, far_branch, middle_late, nffn_late = fence(
        (far_sent, grad_projected, far_branch, grad_middle, grad_normed_ffn)
    )
    far_sum = xor_sp(far_sent, far)

    grad_qkv = dot_tn(normed_all, projected_late).astype(BF)
    my_qkv_bias_grad = jnp.sum(projected_late.astype(F32), axis=0)
    qkv_keep, qkv_send = split_pair(grad_qkv.reshape(-1, 2, n_s * cols, 3 * part_width), 1)
    qkv_arrived = swap_utt(qkv_send)
    branch_blocks, step = [grad_branch, far_branch], n_s // 4
    while step >= 1:
        branch_blocks = branch_blocks + [xor_sp(b, step) for b in branch_blocks]
        step //= 2
    grad_output = dot_tn(attended_heads, jnp.concatenate(branch_blocks, axis=0)).astype(BF)
    grad_output_bias = jnp.sum((gate_attn * middle_late).astype(BF).astype(F32), axis=0)
    early_tables = [
        segment_sums(v) for v in (middle_late * branch, nffn_late, nffn_late * middle_norm)
    ]
    far_sum, early_tables, qkv_keep, qkv_arrived, grad_output = fence(
        (far_sum, early_tables, qkv_keep, qkv_arrived, grad_output)
    )
    grad_normed = kept[:rows] + arrived[:rows].astype(F32) + far_sum.astype(F32)

    grad_base = (
        grad_middle + norm_back(base_norm, base_scale, grad_normed * (1.0 + scale_attn))
    ).astype(BF)
    far_base = xor_sp(grad_base, far)
    far_base, normed_late = fence((far_base, grad_normed))
    two_base = jnp.concatenate([grad_base, far_base], axis=0)
    near_base = xor_sp(two_base, 1)
    grad_skip = dot_tn(
        jnp.concatenate(joined_mine, axis=0), jnp.concatenate([two_base, near_base], axis=0)
    ).astype(BF)
    skip_keep, skip_send = split_pair(grad_skip.reshape((-1, 2) + (slot, width)), 1)
    skip_send, grad_output, base_late, normed_late, result_sent, late_grad = fence(
        (skip_send, grad_output, grad_base, normed_late, result_sent, out_grad)
    )

    skip_arrived, far_result = swap_utt(skip_send), xor_sp(result_sent, far)
    frames_grad = dot_nt(base_late, full_skip[:width])
    skip_grad = dot_nt(base_late, full_skip[width:])
    late_tables = [segment_sums(v) for v in (normed_late, normed_late * base_norm)]
    skip_arrived, far_result, late_tables, frames_grad, skip_grad, qkv_keep, ff_mine = fence(
        (skip_arrived, far_result, late_tables, frames_grad, skip_grad, qkv_keep, ff_mine)
    )
    qkv_half = (qkv_keep.astype(F32) + qkv_arrived.astype(F32)).astype(BF)
    grad_out = late_grad.astype(F32)
    result = (
        result_kept[:rows]
        + result_arrived[:rows].astype(F32)
        + far_result.astype(F32)
        + full_down_bias[None, :]
    )
    skip_half = (skip_keep.astype(F32) + skip_arrived.astype(F32)).astype(BF)
    out_keep, out_send = split_pair(grad_output.reshape(-1, 2, out_slot, width), 1)
    skip_half, qkv_half, out_send = fence((skip_half, qkv_half, out_send))

    skip_terms, qkv_terms = scatter_slow(skip_half), scatter_slow(qkv_half)
    out_arrived = swap_utt(out_send)
    mixed_out = (middle + gate_ffn * result).astype(BF)
    grad_down_bias = jnp.sum((gate_ffn * grad_out).astype(BF).astype(F32), axis=0)
    gate_table = segment_sums(grad_out * result)
    skip_sum = add_terms(skip_terms)
    out_half = (out_keep.astype(F32) + out_arrived.astype(F32)).astype(BF)
    qkv_mine = add_terms(qkv_terms).astype(BF)
    qkv_mine = qkv_mine.reshape(n_s, cols, 3 * part_width)
    out_sum = to_owner(add_terms(scatter_slow(out_half)))
    qkv_back = split_exchange_sp(qkv_mine)
    qkv_sum = (
        qkv_back.reshape(n_s, cols, 3, part_width).transpose(1, 2, 0, 3).reshape(cols, 3 * width)
    ).astype(F32)
    up_back = split_exchange_sp(ff_mine[: n_s * cols].reshape(n_s, cols, part_ff))
    up_sum = (
        up_back.reshape(n_s, cols, n_u, ff // n_all).transpose(1, 2, 0, 3).reshape(cols, ff)
    ).astype(F32)
    down_sum = ff_mine[n_s * cols :].astype(F32)

    grad_table = jnp.concatenate(late_tables + early_tables + [gate_table], axis=1)
    qkv_bias_slots = lax.dynamic_update_slice(
        jnp.zeros((3, width), F32), my_qkv_bias_grad.reshape(3, part_width), (0, s * part_width)
    ).reshape(-1)
    up_bias_slots = lax.dynamic_update_slice(
        jnp.zeros((n_u, n_s, ff // n_all), F32),
        grad_up_bias.reshape(n_u, 1, ff // n_all),
        (0, s, 0),
    ).reshape(-1)
    bias_vec = jnp.concatenate(
        [
            v.reshape(n_u, -1)
            for v in (qkv_bias_slots, grad_output_bias, up_bias_slots, grad_down_bias)
        ],
        axis=1,
    )
    vec_rows = -(-bias_vec.shape[1] // LANES)
    bias_vec = jnp.pad(bias_vec, ((0, 0), (0, vec_rows * LANES - bias_vec.shape[1])))
    table_rows = per_group * table_width // LANES
    tail = jnp.concatenate(
        [grad_table.reshape(table_rows, LANES), bias_vec.reshape(n_u * vec_rows, LANES)], axis=0
    )
    tail = sum_sp(tail)
    tail = jnp.concatenate(
        [
            jnp.broadcast_to(tail[None, :table_rows], (n_u, table_rows, LANES)),
            tail[table_rows:].reshape(n_u, vec_rows, LANES),
        ],
        axis=1,
    )
    tail = tail.astype(BF)
    tail = lax.all_to_all(tail, "utt", 0, 0, tiled=True).astype(F32)
    table_all = tail[:, :table_rows].reshape(n_u * per_group, table_width)
    adaln_sum = lax.dot_general(
        silu_own.astype(F32),
        table_all,
        (((0,), (0,)), ((), ())),
        precision=highest_precision,
        preferred_element_type=F32,
    )
    adaln_bias_sum = jnp.sum(owned(table_all), axis=0)
    vec = jnp.sum(tail[:, table_rows:], axis=0).reshape(-1)
    bias_sums, start = [], 0
    for size in bias_sizes:
        bias_sums.append(lax.dynamic_slice_in_dim(vec, start + s * size, size, 0))
        start += size * n_s

    return (
        mixed_out,
        frames_grad,
        skip_grad,
        skip_sum,
        adaln_sum,
        adaln_bias_sum,
        qkv_sum,
        bias_sums[0],
        out_sum,
        bias_sums[1],
        up_sum,
        bias_sums[2],
        down_sum,
        bias_sums[3],
    )


def solution(mesh):
    both = ("utt", "sp")
    matrix, vector, group = P(both, None), P(both), P("utt", None)
    return jax.shard_map(
        body,
        mesh=mesh,
        in_specs=(
            matrix,
            matrix,
            group,
            group,
            matrix,
            matrix,
            vector,
            matrix,
            vector,
            matrix,
            vector,
            matrix,
            vector,
            matrix,
            vector,
            matrix,
        ),
        out_specs=(
            matrix,
            matrix,
            matrix,
            matrix,
            matrix,
            vector,
            matrix,
            vector,
            matrix,
            vector,
            matrix,
            vector,
            matrix,
            vector,
        ),
        check_vma=False,
    )
```

time: 493 us -> 434 us (0.88)
  matrix products: 103 us -> 24 us
  Pallas kernels: 0 us -> 79 us
  waiting for transfers between devices: 170 us -> 150 us
  other arithmetic: 69.3 us -> 52.7 us
  local copies, waits for them, and re-layouts: 48.9 us -> 36 us
  starting transfers between devices: 74.8 us -> 68.8 us
    pallas_call x0 -> x6, Pallas kernels: none -> 79 us  [the longest x1 20.3 us: feed_forward(): pl.pallas_call(kernel, grid=(steps + 1,), out_shape=(jax.ShapeDtypeStruct...]
    all_to_all x11 -> x5, waiting for transfers between devices: 66.9 us -> 19.7 us  [the longest x1 12.5 us: body(): lax.all_to_all(jnp.broadcast_to(after(output_weight, over_sp)[None], (n_u...]
    dot_general x14 -> x2, matrix products: 41.4 us -> 6.47 us  [product(): lax.dot_general(left, right, (((left_dim,), (right_dim,)), ((), ())), pre...]
    all_to_all x11 -> x5, starting transfers between devices: 46.7 us -> 23.7 us  [the longest x1 6.03 us: body(): mod_terms = lax.all_to_all(mod_terms, 'utt', 0, 0, tiled=True)]
    ppermute x5 -> x17, waiting for transfers between devices: 27.1 us -> 50 us  [the longest x5 27.9 us: swap_utt(): lax.ppermute(values, 'utt', [(i, i ^ 1) for i in range(lax.axis_size('utt...]
    dot_general x6 -> x3, matrix products: 24.2 us -> 5.1 us  [dot_nt(): lax.dot_general(left, right, (((1,), (1,)), ((), ())), preferred_element_...]
    ppermute x5 -> x17, starting transfers between devices: 2.32 us -> 19 us  [the longest x12 16.9 us: turn_utt(): return lax.ppermute(values, 'utt', routes)]
    dot_general x7 -> x2, matrix products: 17 us -> 3.72 us  [dot32(): return jnp.dot(left, right, preferred_element_type=F32)]
  transfers between devices with their start and end apart: 62 -> 67, of which waited for: 26 -> 28; matrix products, arithmetic and copies ran while one was open for 41% -> 21% of each run, Pallas kernels for 0% -> 14%
where the time goes in v2:
time: 434 us; the launch traced here: 427 us
  waiting for transfers between devices  150 us (35%)
  Pallas kernels  79 us (18%)
  starting transfers between devices  68.8 us (16%)
  other arithmetic  52.7 us (12%)
  local copies, waits for them, and re-layouts  36 us (8%)
  matrix products  24 us (6%)
  between operations  16.4 us (4%)
    ppermute x41, waiting for transfers between devices, xor_sp(): return lax.ppermute(values, 'sp', [(i, i ^ distance) for i in range(size)])  71.5 us
    ppermute x5, waiting for transfers between devices, swap_utt(): lax.ppermute(values, 'utt', [(i, i ^ 1) for i in range(lax.axis_size('utt...  27.9 us
    ppermute x41, starting transfers between devices, xor_sp(): return lax.ppermute(values, 'sp', [(i, i ^ distance) for i in range(size)])  23.9 us
    ppermute x12, waiting for transfers between devices, turn_utt(): return lax.ppermute(values, 'utt', routes)  22.1 us
    pallas_call x1, Pallas kernels, feed_forward(): pl.pallas_call(kernel, grid=(steps + 1,), out_shape=(jax.ShapeDtypeStruct...  20.3 us
    pallas_call x1, Pallas kernels, attend_back(): pl.pallas_call(kernel, out_shape=jax.ShapeDtypeStruct((total, 3 * cols),...  18.1 us
    ppermute x12, starting transfers between devices, turn_utt(): return lax.ppermute(values, 'utt', routes)  16.9 us
    pallas_call x1, Pallas kernels, attend(): pl.pallas_call(kernel, out_shape=(jax.ShapeDtypeStruct((total, width), BF...  15.5 us
  transfers between devices with their start and end apart: 67, of which 28 were waited for; matrix products, arithmetic and copies ran while one was open for 21% of the time, Pallas kernels for 14%

profile of v2, /device:TPU:4, one launch (start us, length us, event | category | flops | bytes accessed | tf_op | source)
XLA Modules:
  0.0 426.9 jit_solution(17555993762288934499)
XLA Ops:
  14.8 3.7 all-to-all-start
  21.3 3.4 fusion.2
  26.4 3.5 all-to-all-start.1
  30.9 7.2 %all-to-all-done.1 = bf16[4,32,1792]{2,1,0:T(8,128)(2,1)S(1)} async-done(((bf16[4,32,1792]{2,1,0:T(8,128)(2,1)}), bf16[4,32,1792]{2,1,0:T(8,128)(2,1)S(1)}, u32[]{:S(2)}, u32[]{:S(2)}) %all-to-all-start.1) | async-done | bytes 458784 | tf_op jit(solution)/shard_map/all_to_all | solution.py:815
  43.8 6.0 %all-to-all-start.2 = ((f32[8,18,1024]{2,1,0:T(8,128)}), f32[8,18,1024]{2,1,0:T(8,128)S(1)}, u32[]{:S(2)}, u32[]{:S(2)}) async-start(f32[8,18,1024]{2,1,0:T(8,128)} %copy.107), calls=%async_computation.2 | async-start | bytes 1572864 | tf_op jit(solution)/shard_map/all_to_all | solution.py:849
  56.8 8.4 %collective-permute-done.3.refs_1_ = bf16[256,1024]{1,0:T(8,128)(2,1)} collective-permute-done((bf16[256,1024]{1,0:T(8,128)(2,1)S(1)}, bf16[256,1024]{1,0:T(8,128)(2,1)}, u32[]{:S(2)}, u32[]{:S(2)}) %collective-permute-start.3) | collective-permute-done | bytes 524320 | tf_op jit(solution)/shard_map/ppermute | solution.py:54
  65.2 4.2 collective-permute-done.4.refs_2_
  69.3 5.0 %collective-permute-done.5 = bf16[2,256,512]{2,1,0:T(8,128)(2,1)S(1)} collective-permute-done((bf16[2,256,512]{2,1,0:T(8,128)(2,1)S(1)}, bf16[2,256,512]{2,1,0:T(8,128)(2,1)S(1)}, u32[]{:S(2)}, u32[]{:S(2)}) %collective-permute-start.5) | collective-permute-done | bytes 524320 | tf_op jit(solution)/shard_map/ppermute | solution.py:54
  80.9 6.2 %collective-permute-done.11 = f32[21,1024]{1,0:T(8,128)S(1)} collective-permute-done((f32[21,1024]{1,0:T(8,128)S(1)}, f32[21,1024]{1,0:T(8,128)S(1)}, u32[]{:S(2)}, u32[]{:S(2)}) %collective-permute-start.11) | collective-permute-done | bytes 86048 | tf_op jit(solution)/shard_map/ppermute | solution.py:54
  99.0 5.4 %all-to-all-start.3 = ((bf16[8,32,1024]{2,1,0:T(8,128)(2,1)}), bf16[8,32,1024]{2,1,0:T(8,128)(2,1)S(1)}, u32[]{:S(2)}, u32[]{:S(2)}) async-start(bf16[8,32,1024]{2,1,0:T(8,128)(2,1)} %broadcast_in_dim.392), calls=%async_computation.3 | async-start | bytes 1048576 | tf_op jit(solution)/shard_map/all_to_all | solution.py:861
  104.4 6.2 %placed_product.2 = (bf16[2048,1024]{1,0:T(8,128)(2,1)}, f32[256,1024]{1,0:T(8,128)}) custom-call(s32[40]{0:T(128)} %stack.416.offset_ref, bf16[256,1024]{1,0:T(8,128)(2,1)} %copy-done.23, bf16[256,1024]{1,0:T(8,128)(2,1)} %collective-permute-done.3.refs_1_, bf16[256,1024]{1,0:T(8,128)(2,1)} %collective-permute-done.4.refs_2_, ...), custom_call_target="tpu_custom_call" | custom-call | flops 1073741824 | bytes 10485760 | tf_op jit(solution)/shard_map/placed_product/pallas_call | solution.py:290
  119.4 12.5 %all-to-all-done.3 = bf16[8,32,1024]{2,1,0:T(8,128)(2,1)S(1)} async-done(((bf16[8,32,1024]{2,1,0:T(8,128)(2,1)}), bf16[8,32,1024]{2,1,0:T(8,128)(2,1)S(1)}, u32[]{:S(2)}, u32[]{:S(2)}) %all-to-all-start.3) | async-done | bytes 524320 | tf_op jit(solution)/shard_map/all_to_all | solution.py:861
  140.6 15.5 %attend_forward.1 = (bf16[1024,1024]{1,0:T(8,128)(2,1)}, bf16[1024,256]{1,0:T(8,128)(2,1)}, bf16[1024,256]{1,0:T(8,128)(2,1)}, bf16[1024,256]{1,0:T(8,128)(2,1)}...) custom-call(bf16[512,1024]{1,0:T(8,128)(2,1)} %pad_maximum_fusion.refs_0_, ...), custom_call_target="tpu_custom_call" | custom-call | flops 2684354560 | bytes 5767168 | tf_op jit(solution)/shard_map/attend_forward/pallas_call | solution.py:394
  160.9 3.5 collective-permute-done.19
  167.3 4.6 %placed_product.3 = (bf16[1024,1024]{1,0:T(8,128)(2,1)}, f32[256,1024]{1,0:T(8,128)}) custom-call(s32[32]{0:T(128)} %stack.450.offset_ref, bf16[256,1024]{1,0:T(8,128)(2,1)} %bitcast.258, bf16[256,1024]{1,0:T(8,128)(2,1)} %copy-done.14, bf16[512,1024]{1,0:T(8,128)(2,1)} %collective-permute-done.22.refs_2_, bf16[256,1024]{1,0:T(8,128)(2,1)} %pad_maximum_fusion.11.refs_3_), custom_call_target="tpu_custom_call" | custom-call | flops 536870912 | bytes 5767168 | tf_op jit(solution)/shard_map/placed_product/pallas_call | solution.py:290
  176.8 13.1 %collective-permute-done.24 = bf16[256,1024]{1,0:T(8,128)(2,1)S(1)} collective-permute-done((bf16[256,1024]{1,0:T(8,128)(2,1)S(1)}, bf16[256,1024]{1,0:T(8,128)(2,1)S(1)}, u32[]{:S(2)}, u32[]{:S(2)}) %collective-permute-start.24) | collective-permute-done | bytes 524320 | tf_op jit(solution)/shard_map/ppermute | solution.py:54
  192.8 20.3 %feed_forward.1 = (bf16[1024,1024]{1,0:T(8,128)(2,1)}, bf16[1024,1024]{1,0:T(8,128)(2,1)}, f32[1,1024]{1,0:T(1,128)}, f32[512,1024]{1,0:T(8,128)}, bf16[512,1024]{1,0:T(8,128)(2,1)}) custom-call(bf16[512,1024]{1,0:T(8,128)(2,1)} %copy-done.20, bf16[512,1024]{1,0:T(8,128)(2,1)} %collective-permute-done.25.refs_1_, bf16[256,1024]{1,0:T(8,128)(2,1)} %copy-done.13, ...), custom_call_target="tpu_custom_call" | custom-call | flops 6442450944 | bytes 16777216 | tf_op jit(solution)/shard_map/feed_forward/pallas_call | solution.py:615
  219.9 14.3 %feed_forward_weights.1 = (bf16[8,256,1024]{2,1,0:T(8,128)(2,1)}, f32[512,1024]{1,0:T(8,128)}, bf16[512,1024]{1,0:T(8,128)(2,1)}) custom-call(bf16[512,1024]{1,0:T(8,128)(2,1)} %copy-done.20, bf16[512,1024]{1,0:T(8,128)(2,1)} %collective-permute-done.25.refs_1_, bf16[256,1024]{1,0:T(8,128)(2,1)} %copy-done.13, ...), custom_call_target="tpu_custom_call" | custom-call | flops 6442450944 | bytes 12582912 | tf_op jit(solution)/shard_map/feed_forward_weights/pallas_call | solution.py:712
  243.9 4.2 collective-permute-done.28.refs_6_
  251.1 18.1 %attend_backward.1 = bf16[1024,768]{1,0:T(8,128)(2,1)} custom-call(bf16[1024,256]{1,0:T(8,128)(2,1)} %get-tuple-element.188.refs_0_, bf16[1024,256]{1,0:T(8,128)(2,1)} %get-tuple-element.189.refs_1_, bf16[1024,256]{1,0:T(8,128)(2,1)} %get-tuple-element.190.refs_2_, f32[1024,128]{1,0:T(8,128)} %pad_maximum_fusion.6.refs_3_, ...), custom_call_target="tpu_custom_call" | custom-call | flops 2684354560 | bytes 3670016 | tf_op jit(solution)/shard_map/attend_backward/pallas_call | solution.py:496
  269.2 3.7 convolution_convert_fusion.1
  287.3 4.4 %collective-permute-done.34 = bf16[256,1024]{1,0:T(8,128)(2,1)S(1)} collective-permute-done((bf16[256,1024]{1,0:T(8,128)(2,1)S(1)}, bf16[256,1024]{1,0:T(8,128)(2,1)S(1)}, u32[]{:S(2)}, u32[]{:S(2)}) %collective-permute-start.34) | collective-permute-done | bytes 524320 | tf_op jit(solution)/shard_map/ppermute | solution.py:54
  291.7 15.7 %collective-permute-done.35 = bf16[4,128,768]{2,1,0:T(8,128)(2,1)S(1)} collective-permute-done((bf16[4,128,768]{2,1,0:T(8,128)(2,1)S(1)}, bf16[4,128,768]{2,1,0:T(8,128)(2,1)S(1)}, u32[]{:S(2)}, u32[]{:S(2)}) %collective-permute-start.35) | collective-permute-done | bytes 786464 | tf_op jit(solution)/shard_map/ppermute | solution.py:58
  310.7 12.3 %collective-permute-done.38 = bf16[256,1024]{1,0:T(8,128)(2,1)S(1)} collective-permute-done((bf16[256,1024]{1,0:T(8,128)(2,1)S(1)}, bf16[256,1024]{1,0:T(8,128)(2,1)S(1)}, u32[]{:S(2)}, u32[]{:S(2)}) %collective-permute-start.38) | collective-permute-done | bytes 524320 | tf_op jit(solution)/shard_map/ppermute | solution.py:54
  327.0 2.9 fusion.21
  336.6 7.8 %collective-permute-done.40 = bf16[4,64,1024]{2,1,0:T(8,128)(2,1)} collective-permute-done((bf16[4,64,1024]{2,1,0:T(8,128)(2,1)S(1)}, bf16[4,64,1024]{2,1,0:T(8,128)(2,1)}, u32[]{:S(2)}, u32[]{:S(2)}) %collective-permute-start.40) | collective-permute-done | bytes 524320 | tf_op jit(solution)/shard_map/ppermute | solution.py:58
  357.2 4.8 %collective-permute-done.45 = f32[216,128]{1,0:T(8,128)S(1)} collective-permute-done((f32[216,128]{1,0:T(8,128)S(1)}, f32[216,128]{1,0:T(8,128)S(1)}, u32[]{:S(2)}, u32[]{:S(2)}) %collective-permute-start.45) | collective-permute-done | bytes 110624 | tf_op jit(solution)/shard_map/ppermute | solution.py:54
  369.9 11.5 %collective-permute-done.48 = bf16[128,768]{1,0:T(8,128)(2,1)S(1)} collective-permute-done((bf16[128,768]{1,0:T(8,128)(2,1)S(1)}, bf16[128,768]{1,0:T(8,128)(2,1)S(1)}, u32[]{:S(2)}, u32[]{:S(2)}) %collective-permute-start.48) | collective-permute-done | bytes 196640 | tf_op jit(solution)/shard_map/ppermute | solution.py:95
  384.0 5.1 %all-to-all-start.4 = ((bf16[8,153,128]{2,1,0:T(8,128)(2,1)}), bf16[8,153,128]{2,1,0:T(8,128)(2,1)S(1)}, u32[]{:S(2)}, u32[]{:S(2)}) async-start(bf16[8,153,128]{2,1,0:T(8,128)(2,1)} %pad_maximum_fusion.14), calls=%async_computation.5 | async-start | bytes 655360 | tf_op jit(solution)/shard_map/all_to_all | solution.py:1128
  389.2 3.3 collective-permute-start.55
  397.0 7.4 %collective-permute-done.54 = bf16[32,1024]{1,0:T(8,128)(2,1)S(1)} collective-permute-done((bf16[32,1024]{1,0:T(8,128)(2,1)S(1)}, bf16[32,1024]{1,0:T(8,128)(2,1)S(1)}, u32[]{:S(2)}, u32[]{:S(2)}) %collective-permute-start.54) | collective-permute-done | bytes 65568 | tf_op jit(solution)/shard_map/ppermute | solution.py:95
  407.9 7.2 %collective-permute-done.56 = f32[32,1024]{1,0:T(8,128)S(1)} collective-permute-done((f32[32,1024]{1,0:T(8,128)S(1)}, f32[32,1024]{1,0:T(8,128)S(1)}, u32[]{:S(2)}, u32[]{:S(2)}) %collective-permute-start.56) | collective-permute-done | bytes 131104 | tf_op jit(solution)/shard_map/ppermute | solution.py:208
  (536 shorter events, 159.5 us)
Async XLA Ops:
  7.2 23.6 %collective-permute-start = (bf16[64,1024]{1,0:T(8,128)(2,1)}, bf16[64,1024]{1,0:T(8,128)(2,1)S(1)}, u32[]{:S(2)}, u32[]{:S(2)}) collective-permute-start(bf16[64,1024]{1,0:T(8,128)(2,1)} %param.20), channel_id=1, source_target_pairs={{0,8},{4,12},{8,16},{12,20},{16,24},{20,28},{24,0},{28,4},{1,9},{5... | collective-permute-start | bytes 393224 | tf_op jit(solution)/shard_map/ppermute | solution.py:95
  8.9 22.0 %collective-permute-start.1 = (bf16[64,1024]{1,0:T(8,128)(2,1)}, bf16[64,1024]{1,0:T(8,128)(2,1)S(1)}, u32[]{:S(2)}, u32[]{:S(2)}) collective-permute-start(bf16[64,1024]{1,0:T(8,128)(2,1)} %param.20), channel_id=1, source_target_pairs={{0,16},{4,20},{8,24},{12,28},{16,0},{20,4},{24,8},{28,12},{1,17},{... | collective-permute-start | bytes 393224 | tf_op jit(solution)/shard_map/ppermute | solution.py:95
  11.4 19.4 %collective-permute-start.2 = (bf16[64,1024]{1,0:T(8,128)(2,1)}, bf16[64,1024]{1,0:T(8,128)(2,1)S(1)}, u32[]{:S(2)}, u32[]{:S(2)}) collective-permute-start(bf16[64,1024]{1,0:T(8,128)(2,1)} %param.20), channel_id=1, source_target_pairs={{0,24},{4,28},{8,0},{12,4},{16,8},{20,12},{24,16},{28,20},{1,25},{... | collective-permute-start | bytes 393224 | tf_op jit(solution)/shard_map/ppermute | solution.py:95
  29.9 59.0 %all-gather.4.cloned.1.call-start = ((), (), s32[]{:S(2)}) async-start(), calls=%async_computation.6 | async-start | bytes 1769472 | tf_op jit(solution)/shard_map/all_gather | solution.py:828
  43.8 31.4 %all-to-all-start.2 = ((f32[8,18,1024]{2,1,0:T(8,128)}), f32[8,18,1024]{2,1,0:T(8,128)S(1)}, u32[]{:S(2)}, u32[]{:S(2)}) async-start(f32[8,18,1024]{2,1,0:T(8,128)} %copy.107), calls=%async_computation.2 | async-start | bytes 1572864 | tf_op jit(solution)/shard_map/all_to_all | solution.py:849
  49.8 141.0 %all-gather.6.cloned.1.call-start = ((), (), s32[]{:S(2)}) async-start(), calls=%async_computation.8 | async-start | bytes 4718592 | tf_op jit(solution)/shard_map/all_gather | solution.py:829
  50.1 15.0 %collective-permute-start.3 = (bf16[256,1024]{1,0:T(8,128)(2,1)S(1)}, bf16[256,1024]{1,0:T(8,128)(2,1)}, u32[]{:S(2)}, u32[]{:S(2)}) collective-permute-start(bf16[256,1024]{1,0:T(8,128)(2,1)S(1)} %constant_dynamic-update-slice_fusion.refs_0_), channel_id=1, source_target_pairs={{0,2},{1,3},{2,0},{3,1},{4,6},{5,7},{6,4},{7,5},{8,10},{9,11},{10,... | collective-permute-start | bytes 1572872 | tf_op jit(solution)/shard_map/ppermute | solution.py:54
  50.5 18.8 %collective-permute-start.4 = (bf16[256,1024]{1,0:T(8,128)(2,1)S(1)}, bf16[256,1024]{1,0:T(8,128)(2,1)}, u32[]{:S(2)}, u32[]{:S(2)}) collective-permute-start(bf16[256,1024]{1,0:T(8,128)(2,1)S(1)} %constant_dynamic-update-slice_fusion.refs_0_), channel_id=1, source_target_pairs={{0,4},{4,0},{8,12},{12,8},{16,20},{20,16},{24,28},{28,24},{1,5},{5... | collective-permute-start | bytes 1572872 | tf_op jit(solution)/shard_map/ppermute | solution.py:58
  50.6 24.5 %collective-permute-start.6 = (bf16[256,1024]{1,0:T(8,128)(2,1)S(1)}, bf16[256,1024]{1,0:T(8,128)(2,1)}, u32[]{:S(2)}, u32[]{:S(2)}) collective-permute-start(bf16[256,1024]{1,0:T(8,128)(2,1)S(1)} %constant_dynamic-update-slice_fusion.refs_0_), channel_id=1, source_target_pairs={{0,1},{1,0},{2,3},{3,2},{4,5},{5,4},{6,7},{7,6},{8,9},{9,8},{10,11... | collective-permute-start | bytes 1572872 | tf_op jit(solution)/shard_map/ppermute | solution.py:54
  50.6 23.7 %collective-permute-start.5 = (bf16[2,256,512]{2,1,0:T(8,128)(2,1)S(1)}, bf16[2,256,512]{2,1,0:T(8,128)(2,1)S(1)}, u32[]{:S(2)}, u32[]{:S(2)}) collective-permute-start(bf16[2,256,512]{2,1,0:T(8,128)(2,1)S(1)} %copy-done.32), channel_id=1, source_target_pairs={{0,2},{1,3},{2,0},{3,1},{4,6},{5,7},{6,4},{7,5},{8,10},{9,11},{10,... | collective-permute-start | bytes 1572872 | tf_op jit(solution)/shard_map/ppermute | solution.py:54
  93.3 17.4 %collective-permute-start.14 = (bf16[256,1024]{1,0:T(8,128)(2,1)S(1)}, bf16[256,1024]{1,0:T(8,128)(2,1)}, u32[]{:S(2)}, u32[]{:S(2)}) collective-permute-start(bf16[256,1024]{1,0:T(8,128)(2,1)S(1)} %fusion.27.refs_2_), channel_id=1, source_target_pairs={{0,2},{1,3},{2,0},{3,1},{4,6},{5,7},{6,4},{7,5},{8,10},{9,11},{10,... | collective-permute-start | bytes 1572872 | tf_op jit(solution)/shard_map/ppermute | solution.py:54
  99.0 33.0 %all-to-all-start.3 = ((bf16[8,32,1024]{2,1,0:T(8,128)(2,1)}), bf16[8,32,1024]{2,1,0:T(8,128)(2,1)S(1)}, u32[]{:S(2)}, u32[]{:S(2)}) async-start(bf16[8,32,1024]{2,1,0:T(8,128)(2,1)} %broadcast_in_dim.392), calls=%async_computation.3 | async-start | bytes 1048576 | tf_op jit(solution)/shard_map/all_to_all | solution.py:861
  104.4 240.3 %reduce-scatter.2.cloned.1.call-start = ((), (), s32[]{:S(2)}) async-start(), calls=%async_computation.7 | async-start | bytes 4718592 | tf_op jit(solution)/shard_map/reduce_scatter | solution.py:995
  115.1 16.9 %collective-permute-start.15 = (bf16[256,1024]{1,0:T(8,128)(2,1)S(1)}, bf16[256,1024]{1,0:T(8,128)(2,1)}, u32[]{:S(2)}, u32[]{:S(2)}) collective-permute-start(bf16[256,1024]{1,0:T(8,128)(2,1)S(1)} %add_convert_fusion.6), channel_id=1, source_target_pairs={{0,2},{1,3},{2,0},{3,1},{4,6},{5,7},{6,4},{7,5},{8,10},{9,11},{10,... | collective-permute-start | bytes 1572872 | tf_op jit(solution)/shard_map/ppermute | solution.py:54
  118.4 15.8 %collective-permute-start.17 = (bf16[2,256,512]{2,1,0:T(8,128)(2,1)}, bf16[2,256,512]{2,1,0:T(8,128)(2,1)}, u32[]{:S(2)}, u32[]{:S(2)}) collective-permute-start(bf16[2,256,512]{2,1,0:T(8,128)(2,1)} %pad_maximum_fusion.9), channel_id=1, source_target_pairs={{0,1},{1,0},{2,3},{3,2},{4,5},{5,4},{6,7},{7,6},{8,9},{9,8},{10,11... | collective-permute-start | bytes 1572872 | tf_op jit(solution)/shard_map/ppermute | solution.py:54
  137.2 18.9 %collective-permute-start.18 = (bf16[256,1024]{1,0:T(8,128)(2,1)S(1)}, bf16[256,1024]{1,0:T(8,128)(2,1)S(1)}, u32[]{:S(2)}, u32[]{:S(2)}) collective-permute-start(bf16[256,1024]{1,0:T(8,128)(2,1)S(1)} %bitcast.256), channel_id=1, source_target_pairs={{0,2},{1,3},{2,0},{3,1},{4,6},{5,7},{6,4},{7,5},{8,10},{9,11},{10,... | collective-permute-start | bytes 1572872 | tf_op jit(solution)/shard_map/ppermute | solution.py:54
  140.2 20.7 %collective-permute-start.23 = (bf16[512,1024]{1,0:T(8,128)(2,1)}, bf16[512,1024]{1,0:T(8,128)(2,1)}, u32[]{:S(2)}, u32[]{:S(2)}) collective-permute-start(bf16[512,1024]{1,0:T(8,128)(2,1)} %pad_maximum_fusion.2), channel_id=1, source_target_pairs={{0,1},{1,0},{2,3},{3,2},{4,5},{5,4},{6,7},{7,6},{8,9},{9,8},{10,11... | collective-permute-start | bytes 3145736 | tf_op jit(solution)/shard_map/ppermute | solution.py:54
  175.3 14.6 %collective-permute-start.24 = (bf16[256,1024]{1,0:T(8,128)(2,1)S(1)}, bf16[256,1024]{1,0:T(8,128)(2,1)S(1)}, u32[]{:S(2)}, u32[]{:S(2)}) collective-permute-start(bf16[256,1024]{1,0:T(8,128)(2,1)S(1)} %add_convert_fusion.5), channel_id=1, source_target_pairs={{0,2},{1,3},{2,0},{3,1},{4,6},{5,7},{6,4},{7,5},{8,10},{9,11},{10,... | collective-permute-start | bytes 1572872 | tf_op jit(solution)/shard_map/ppermute | solution.py:54
  218.2 16.0 %collective-permute-start.27 = (bf16[256,1024]{1,0:T(8,128)(2,1)}, bf16[256,1024]{1,0:T(8,128)(2,1)}, u32[]{:S(2)}, u32[]{:S(2)}) collective-permute-start(bf16[256,1024]{1,0:T(8,128)(2,1)} %add_convert_fusion.4), channel_id=1, source_target_pairs={{0,2},{1,3},{2,0},{3,1},{4,6},{5,7},{6,4},{7,5},{8,10},{9,11},{10,... | collective-permute-start | bytes 1572872 | tf_op jit(solution)/shard_map/ppermute | solution.py:54
  250.7 18.5 %collective-permute-start.32 = (bf16[256,1024]{1,0:T(8,128)(2,1)}, bf16[256,1024]{1,0:T(8,128)(2,1)}, u32[]{:S(2)}, u32[]{:S(2)}) collective-permute-start(bf16[256,1024]{1,0:T(8,128)(2,1)} %copy-done.37), channel_id=1, source_target_pairs={{0,2},{1,3},{2,0},{3,1},{4,6},{5,7},{6,4},{7,5},{8,10},{9,11},{10,... | collective-permute-start | bytes 1572872 | tf_op jit(solution)/shard_map/ppermute | solution.py:54
  277.7 14.0 %collective-permute-start.34 = (bf16[256,1024]{1,0:T(8,128)(2,1)S(1)}, bf16[256,1024]{1,0:T(8,128)(2,1)S(1)}, u32[]{:S(2)}, u32[]{:S(2)}) collective-permute-start(bf16[256,1024]{1,0:T(8,128)(2,1)S(1)} %fusion.29), channel_id=1, source_target_pairs={{0,2},{1,3},{2,0},{3,1},{4,6},{5,7},{6,4},{7,5},{8,10},{9,11},{10,... | collective-permute-start | bytes 1572872 | tf_op jit(solution)/shard_map/ppermute | solution.py:54
  282.5 24.9 %collective-permute-start.35 = (bf16[4,128,768]{2,1,0:T(8,128)(2,1)S(1)}, bf16[4,128,768]{2,1,0:T(8,128)(2,1)S(1)}, u32[]{:S(2)}, u32[]{:S(2)}) collective-permute-start(bf16[4,128,768]{2,1,0:T(8,128)(2,1)S(1)} %get-tuple-element.279), channel_id=1, source_target_pairs={{0,4},{4,0},{8,12},{12,8},{16,20},{20,16},{24,28},{28,24},{1,5},{5... | collective-permute-start | bytes 2359304 | tf_op jit(solution)/shard_map/ppermute | solution.py:58
  330.0 14.5 %collective-permute-start.40 = (bf16[4,64,1024]{2,1,0:T(8,128)(2,1)S(1)}, bf16[4,64,1024]{2,1,0:T(8,128)(2,1)}, u32[]{:S(2)}, u32[]{:S(2)}) collective-permute-start(bf16[4,64,1024]{2,1,0:T(8,128)(2,1)S(1)} %dynamic-slice_bitcast_fusion.2), channel_id=1, source_target_pairs={{0,4},{4,0},{8,12},{12,8},{16,20},{20,16},{24,28},{28,24},{1,5},{5... | collective-permute-start | bytes 1572872 | tf_op jit(solution)/shard_map/ppermute | solution.py:58
  330.6 14.0 %collective-permute-start.41 = (bf16[256,1024]{1,0:T(8,128)(2,1)S(1)}, bf16[256,1024]{1,0:T(8,128)(2,1)S(1)}, u32[]{:S(2)}, u32[]{:S(2)}) collective-permute-start(bf16[256,1024]{1,0:T(8,128)(2,1)S(1)} %copy-done.33), channel_id=1, source_target_pairs={{0,2},{1,3},{2,0},{3,1},{4,6},{5,7},{6,4},{7,5},{8,10},{9,11},{10,... | collective-permute-start | bytes 1572872 | tf_op jit(solution)/shard_map/ppermute | solution.py:54
  350.5 14.6 %collective-permute-start.44 = (bf16[64,1024]{1,0:T(8,128)(2,1)}, bf16[64,1024]{1,0:T(8,128)(2,1)S(1)}, u32[]{:S(2)}, u32[]{:S(2)}) collective-permute-start(bf16[64,1024]{1,0:T(8,128)(2,1)} %get-tuple-element.293), channel_id=1, source_target_pairs={{0,24},{4,28},{8,0},{12,4},{16,8},{20,12},{24,16},{28,20},{1,25},{... | collective-permute-start | bytes 393224 | tf_op jit(solution)/shard_map/ppermute | solution.py:95
  352.9 13.7 %collective-permute-start.42 = (bf16[64,1024]{1,0:T(8,128)(2,1)S(1)}, bf16[64,1024]{1,0:T(8,128)(2,1)}, u32[]{:S(2)}, u32[]{:S(2)}) collective-permute-start(bf16[64,1024]{1,0:T(8,128)(2,1)S(1)} %get-tuple-element.292), channel_id=1, source_target_pairs={{0,8},{4,12},{8,16},{12,20},{16,24},{20,28},{24,0},{28,4},{1,9},{5... | collective-permute-start | bytes 393224 | tf_op jit(solution)/shard_map/ppermute | solution.py:95
  364.5 16.9 %collective-permute-start.48 = (bf16[128,768]{1,0:T(8,128)(2,1)S(1)}, bf16[128,768]{1,0:T(8,128)(2,1)S(1)}, u32[]{:S(2)}, u32[]{:S(2)}) collective-permute-start(bf16[128,768]{1,0:T(8,128)(2,1)S(1)} %get-tuple-element.289), channel_id=1, source_target_pairs={{0,16},{4,20},{8,24},{12,28},{16,0},{20,4},{24,8},{28,12},{1,17},{... | collective-permute-start | bytes 589832 | tf_op jit(solution)/shard_map/ppermute | solution.py:95
  365.2 16.3 %collective-permute-start.47 = (bf16[128,768]{1,0:T(8,128)(2,1)S(1)}, bf16[128,768]{1,0:T(8,128)(2,1)S(1)}, u32[]{:S(2)}, u32[]{:S(2)}) collective-permute-start(bf16[128,768]{1,0:T(8,128)(2,1)S(1)} %get-tuple-element.287), channel_id=1, source_target_pairs={{0,8},{4,12},{8,16},{12,20},{16,24},{20,28},{24,0},{28,4},{1,9},{5... | collective-permute-start | bytes 589832 | tf_op jit(solution)/shard_map/ppermute | solution.py:95
  365.5 23.6 %collective-permute-start.52 = (bf16[4,32,1024]{2,1,0:T(8,128)(2,1)S(1)}, bf16[4,32,1024]{2,1,0:T(8,128)(2,1)S(1)}, u32[]{:S(2)}, u32[]{:S(2)}) collective-permute-start(bf16[4,32,1024]{2,1,0:T(8,128)(2,1)S(1)} %copy-done.41), channel_id=1, source_target_pairs={{0,4},{4,0},{8,12},{12,8},{16,20},{20,16},{24,28},{28,24},{1,5},{5... | collective-permute-start | bytes 786440 | tf_op jit(solution)/shard_map/ppermute | solution.py:58
  366.6 16.5 %collective-permute-start.46 = (f32[216,128]{1,0:T(8,128)S(1)}, f32[216,128]{1,0:T(8,128)S(1)}, u32[]{:S(2)}, u32[]{:S(2)}) collective-permute-start(f32[216,128]{1,0:T(8,128)S(1)} %add.821), channel_id=1, source_target_pairs={{0,1},{1,0},{2,3},{3,2},{4,5},{5,4},{6,7},{7,6},{8,9},{9,8},{10,11... | collective-permute-start | bytes 331784 | tf_op jit(solution)/shard_map/ppermute | solution.py:54
  369.9 23.8 %collective-permute-start.58 = (bf16[2,32,1024]{2,1,0:T(8,128)(2,1)S(1)}, bf16[2,32,1024]{2,1,0:T(8,128)(2,1)S(1)}, u32[]{:S(2)}, u32[]{:S(2)}) collective-permute-start(bf16[2,32,1024]{2,1,0:T(8,128)(2,1)S(1)} %pad_maximum_fusion.18), channel_id=1, source_target_pairs={{0,1},{1,0},{2,3},{3,2},{4,5},{5,4},{6,7},{7,6},{8,9},{9,8},{10,11... | collective-permute-start | bytes 393224 | tf_op jit(solution)/shard_map/ppermute | solution.py:54
  384.0 31.1 %all-to-all-start.4 = ((bf16[8,153,128]{2,1,0:T(8,128)(2,1)}), bf16[8,153,128]{2,1,0:T(8,128)(2,1)S(1)}, u32[]{:S(2)}, u32[]{:S(2)}) async-start(bf16[8,153,128]{2,1,0:T(8,128)(2,1)} %pad_maximum_fusion.14), calls=%async_computation.5 | async-start | bytes 655360 | tf_op jit(solution)/shard_map/all_to_all | solution.py:1128
  (146 other events, 1389.9 us)
Sparse Core Ops, SparseCore 0:
  38.8 50.0 all-gather.3
  97.5 80.6 all-gather.5
  251.2 92.6 reduce-scatter.1
